TPU v7x, 256 devices: a whole 4x4x8 slice. The times are simulated.
256 devices in a mesh: row: 8 (over z), col: 32 (over y, x, core).
Axes of the slice: x: 4, y: 4, z: 8, core: 2. Of those that a mesh axis runs over, the one named last changes fastest.
Arguments:
- factor_tiles: bfloat16 [3, 96, 64, 2048], P(None, 'row', None, 'col'), may hold values from -0.3125 to 0.3125
- tile_row: int32 [3, 96, 32], P(None, 'row', 'col'), may hold values from 0 to 63
- tile_col: int32 [3, 96, 32], P(None, 'row', 'col'), may hold values from 0 to 15
- right_sides: float32 [4, 512, 64, 128], P(None, ('col', 'row')), may hold values from -6 to 6
- diag_inverse: float32 [4, 64, 32768], P(None, None, ('col', 'row')), as said below
Outputs:
- preconditioned: float32 [4, 512, 64, 128], P(None, ('col', 'row'))
Inputs may be any that keep to these rules, and one draw needn't show every extreme that they name: `tile_row`: a block row within its row group. `tile_col`: a block column within its column group. `diag_inverse`: diagonal entries of every block between 0.5 and 2.
All inputs are finite; a program needn't handle non-finite values.
Results may differ from a plain program's by a relative error of at most 0.025.
Values may be sent and summed in bfloat16 or wider, within the bound.
A program may use at most 64 MiB of HBM per device.

v0:
```python
import jax
import jax.numpy as jnp
from jax import lax
from jax.sharding import PartitionSpec as P


def apply_inverse(inverse, vector, transposed):
    matrix = inverse.reshape(inverse.shape[0], -1, inverse.shape[0])
    if transposed:
        return jnp.einsum("cir,irn->icn", matrix, vector, precision=lax.Precision.HIGHEST)
    return jnp.einsum("cir,icn->irn", matrix, vector, precision=lax.Precision.HIGHEST)


def solve_all(factor_tiles, tile_row, tile_col, right_sides, diag_inverse):
    levels = factor_tiles.shape[0]
    rows_dev = right_sides.shape[1]
    group_rows = rows_dev * lax.axis_size("row")
    row_ids = tile_row[:, :, 0]
    col_ids = tile_col[:, :, 0]
    current = apply_inverse(diag_inverse[0], right_sides[0], False)
    solved = [current]
    for section_no in range(1, levels + 1):
        gathered = lax.all_gather(current.astype(jnp.bfloat16), "row", axis=0, tiled=True)
        picked = gathered[col_ids[section_no - 1]]
        products = jnp.einsum(
            "tab,tbn->tan", factor_tiles[section_no - 1], picked, preferred_element_type=jnp.float32
        )
        targets = row_ids[section_no - 1]

        def term(offset, length, products=products, targets=targets):
            places = jnp.arange(length, dtype=jnp.int32)
            select = (targets[:, None] == places[None, :]).astype(jnp.float32)
            return jnp.einsum("tq,tan->qan", select, products, precision=lax.Precision.HIGHEST)

        row_sums = lax.psum_scatter(
            term(jnp.int32(0), lax.axis_size("col") * rows_dev).astype(jnp.bfloat16),
            "col",
            scatter_dimension=0,
            tiled=True,
        ).astype(jnp.float32)
        current = apply_inverse(diag_inverse[section_no], right_sides[section_no] - row_sums, False)
        solved.append(current)
    current = apply_inverse(diag_inverse[levels], solved[levels], True)
    result = [current]
    columns_here = jnp.arange(group_rows, dtype=jnp.int32)
    for section_no in range(levels - 1, -1, -1):
        everyone = lax.all_gather(current.astype(jnp.bfloat16), "col", axis=0, tiled=True)
        picked = everyone[row_ids[section_no]]
        spread = jnp.einsum(
            "tab,tan->tbn", factor_tiles[section_no], picked, preferred_element_type=jnp.float32
        )
        select = (col_ids[section_no][:, None] == columns_here[None, :]).astype(jnp.float32)
        column_sums = jnp.einsum("tj,tbn->jbn", select, spread, precision=lax.Precision.HIGHEST)
        received = lax.psum_scatter(
            column_sums.astype(jnp.bfloat16), "row", scatter_dimension=0, tiled=True
        ).astype(jnp.float32)
        current = apply_inverse(diag_inverse[section_no], solved[section_no] - received, True)
        result.insert(0, current)
    return jnp.stack(result)


def on_device(factor_tiles, tile_row, tile_col, right_sides, diag_inverse):
    return solve_all(factor_tiles, tile_row, tile_col, right_sides, diag_inverse)


def solution(mesh):
    return jax.shard_map(
        on_device,
        mesh=mesh,
        in_specs=(
            P(None, "row", None, "col"),
            P(None, "row", "col"),
            P(None, "row", "col"),
            P(None, ("col", "row"), None, None),
            P(None, None, ("col", "row")),
        ),
        out_specs=P(None, ("col", "row"), None, None),
        check_vma=False,
    )
```

profile of v0, /device:TPU:1, one launch (start us, length us, event | category | flops | bytes accessed | tf_op | source)
XLA Modules:
  0.0 626.1 jit_solution(13500943562827002383)
XLA Ops:
  6.5 0.9 fusion.66
  7.4 0.1 copy.45
  7.5 1.0 fusion.67
  8.6 23.3 %all_gather.18 = bf16[16,64,128]{2,1,0:T(8,128)(2,1)S(1)} all-gather(bf16[2,64,128]{2,1,0:T(8,128)(2,1)S(1)} %get-tuple-element.21), channel_id=1, replica_groups=mesh['row'=8,'col'=32] {'row'}, dimensions={0}, use_global_device_ids=true | all-gather | bytes 294912 | tf_op jit(solution)/shard_map/all_gather | solution.py:23
  31.8 0.7 fusion.62
  32.5 0.7 slice_bitcast_fusion
  33.2 0.6 gather_fusion
  33.8 0.2 convolution_bitcast_fusion.2
  34.0 1.1 convolution_convert_fusion.2
  35.1 1.7 copy.47
  36.8 0.0 reduce-scatter.7.cloned.1.call-update
  36.8 0.0 reduce-scatter.9.cloned.1.call-start
  36.9 0.1 copy.48
  37.0 88.9 %reduce-scatter.7.cloned.1.call-done = bf16[2,64,128]{2,1,0:T(8,128)(2,1)} async-done(((bf16[64,64,128]{2,1,0:T(8,128)(2,1)}), bf16[2,64,128]{2,1,0:T(8,128)(2,1)}) %reduce-scatter.7.cloned.1.call-update) | async-done | bytes 32784 | tf_op jit(solution)/shard_map/reduce_scatter | solution.py:35
  125.9 1.0 fusion.68
  126.8 20.0 %all_gather.19 = bf16[16,64,128]{2,1,0:T(8,128)(2,1)S(1)} all-gather(bf16[2,64,128]{2,1,0:T(8,128)(2,1)S(1)} %get-tuple-element.23), channel_id=1, replica_groups=mesh['row'=8,'col'=32] {'row'}, dimensions={0}, use_global_device_ids=true | all-gather | bytes 294912 | tf_op jit(solution)/shard_map/all_gather | solution.py:23
  146.9 0.6 gather_fusion.1
  147.4 0.2 convolution_bitcast_fusion.1
  147.6 1.1 convolution_convert_fusion.1
  148.8 1.7 copy.50
  150.4 0.0 reduce-scatter.11.cloned.1.call-start
  150.5 0.1 copy.51
  150.6 89.4 %reduce-scatter.9.cloned.1.call-done = bf16[2,64,128]{2,1,0:T(8,128)(2,1)} async-done(((bf16[64,64,128]{2,1,0:T(8,128)(2,1)}), bf16[2,64,128]{2,1,0:T(8,128)(2,1)}) %reduce-scatter.9.cloned.1.call-update) | async-done | bytes 32784 | tf_op jit(solution)/shard_map/reduce_scatter | solution.py:35
  240.1 1.0 fusion.69
  241.0 20.2 %all_gather.20 = bf16[16,64,128]{2,1,0:T(8,128)(2,1)S(1)} all-gather(bf16[2,64,128]{2,1,0:T(8,128)(2,1)S(1)} %get-tuple-element.25), channel_id=1, replica_groups=mesh['row'=8,'col'=32] {'row'}, dimensions={0}, use_global_device_ids=true | all-gather | bytes 294912 | tf_op jit(solution)/shard_map/all_gather | solution.py:23
  261.2 0.6 gather_fusion.2
  261.8 0.2 convolution_bitcast_fusion
  262.0 1.1 convolution_convert_fusion
  263.1 1.7 copy.53
  264.8 0.0 reduce-scatter.11.cloned.1.call-update
  264.8 0.0 all-gather.4.cloned.1.call-start
  264.8 0.1 reshape_squeeze.19
  264.9 89.3 %reduce-scatter.11.cloned.1.call-done = bf16[2,64,128]{2,1,0:T(8,128)(2,1)} async-done(((bf16[64,64,128]{2,1,0:T(8,128)(2,1)}), bf16[2,64,128]{2,1,0:T(8,128)(2,1)}) %reduce-scatter.11.cloned.1.call-update) | async-done | bytes 32784 | tf_op jit(solution)/shard_map/reduce_scatter | solution.py:35
  354.2 1.0 fusion.21
  355.3 0.8 bitcast_convert_fusion.2
  356.1 0.0 all-gather.4.cloned.1.call-update
  356.1 0.0 reduce-scatter.13.cloned.1.call-start
  356.2 50.0 %all-gather.4.cloned.1.call-done = bf16[64,64,128]{2,1,0:T(8,128)(2,1)} async-done(((bf16[2,64,128]{2,1,0:T(8,128)(2,1)}), bf16[64,64,128]{2,1,0:T(8,128)(2,1)}) %all-gather.4.cloned.1.call-update) | async-done | bytes 1048592 | tf_op jit(solution)/shard_map/all_gather | solution.py:47
  406.3 1.8 gather_fusion.3
  408.1 0.3 convolution_bitcast_fusion.5
  408.3 0.6 fusion.4
  408.9 0.8 copy.95
  409.7 0.0 reduce-scatter.13.cloned.1.call-update
  409.7 0.0 all-gather.6.cloned.1.call-start
  409.8 30.2 %reduce-scatter.13.cloned.1.call-done = bf16[2,64,128]{2,1,0:T(8,128)(2,1)} async-done(((bf16[16,64,128]{2,1,0:T(8,128)(2,1)}), bf16[2,64,128]{2,1,0:T(8,128)(2,1)}) %reduce-scatter.13.cloned.1.call-update) | async-done | bytes 32784 | tf_op jit(solution)/shard_map/reduce_scatter | solution.py:54
  440.0 1.7 bitcast_convert_fusion.1
  441.7 0.0 reduce-scatter.15.cloned.1.call-start
  441.8 53.1 %all-gather.6.cloned.1.call-done = bf16[64,64,128]{2,1,0:T(8,128)(2,1)} async-done(((bf16[2,64,128]{2,1,0:T(8,128)(2,1)}), bf16[64,64,128]{2,1,0:T(8,128)(2,1)}) %all-gather.6.cloned.1.call-update) | async-done | bytes 1048592 | tf_op jit(solution)/shard_map/all_gather | solution.py:47
  494.9 1.8 gather_fusion.4
  496.7 0.3 convolution_bitcast_fusion.4
  497.0 0.6 fusion.2
  497.6 0.8 copy.94
  498.4 0.0 all-gather.8.cloned.1.call-start
  498.4 30.5 %reduce-scatter.15.cloned.1.call-done = bf16[2,64,128]{2,1,0:T(8,128)(2,1)} async-done(((bf16[16,64,128]{2,1,0:T(8,128)(2,1)}), bf16[2,64,128]{2,1,0:T(8,128)(2,1)}) %reduce-scatter.15.cloned.1.call-update) | async-done | bytes 32784 | tf_op jit(solution)/shard_map/reduce_scatter | solution.py:54
  528.9 1.7 bitcast_convert_fusion
  530.6 0.0 reduce-scatter.17.cloned.1.call-start
  530.7 53.4 %all-gather.8.cloned.1.call-done = bf16[64,64,128]{2,1,0:T(8,128)(2,1)} async-done(((bf16[2,64,128]{2,1,0:T(8,128)(2,1)}), bf16[64,64,128]{2,1,0:T(8,128)(2,1)}) %all-gather.8.cloned.1.call-update) | async-done | bytes 1048592 | tf_op jit(solution)/shard_map/all_gather | solution.py:47
  584.0 1.8 gather_fusion.5
  585.9 0.3 convolution_bitcast_fusion.3
  586.1 0.6 fusion
  586.7 0.8 copy.93
  587.5 30.3 %reduce-scatter.17.cloned.1.call-done = bf16[2,64,128]{2,1,0:T(8,128)(2,1)} async-done(((bf16[16,64,128]{2,1,0:T(8,128)(2,1)}), bf16[2,64,128]{2,1,0:T(8,128)(2,1)}) %reduce-scatter.17.cloned.1.call-update) | async-done | bytes 32784 | tf_op jit(solution)/shard_map/reduce_scatter | solution.py:54
  617.8 1.0 convolution_bitcast_fusion.6
  618.8 0.7 pad_maximum_fusion
  (22 shorter events, 0.1 us)
Async XLA Ops:
  6.5 27.3 %copy-start = (bf16[3,12,64,64]{3,2,1,0:T(8,128)(2,1)S(1)}, bf16[3,12,64,64]{3,2,1,0:T(8,128)(2,1)}, u32[]{:S(2)}) copy-start(bf16[3,12,64,64]{3,2,1,0:T(8,128)(2,1)} %param.5) | copy-start | bytes 884740
  6.5 119.3 %reduce-scatter.7.cloned.1.call-start = ((), (), s32[]{:S(2)}) async-start(), calls=%async_computation.6 | async-start | bytes 1081344 | tf_op jit(solution)/shard_map/reduce_scatter | solution.py:35
  36.8 89.1 %copy-start.1 = (f32[4,2,64,128]{3,2,1,0:T(8,128)S(1)}, f32[4,2,64,128]{3,2,1,0:T(8,128)}, u32[]{:S(2)}) copy-start(f32[4,2,64,128]{3,2,1,0:T(8,128)} %param.8) | copy-start | bytes 786436
  36.8 203.2 %reduce-scatter.9.cloned.1.call-start = ((), (), s32[]{:S(2)}) async-start(), calls=%async_computation.7 | async-start | bytes 1081344 | tf_op jit(solution)/shard_map/reduce_scatter | solution.py:35
  150.4 203.8 %reduce-scatter.11.cloned.1.call-start = ((), (), s32[]{:S(2)}) async-start(), calls=%async_computation.8 | async-start | bytes 1081344 | tf_op jit(solution)/shard_map/reduce_scatter | solution.py:35
  264.8 91.4 %copy-start.2 = (s32[3,12,1]{1,2,0:T(1,128)S(1)}, s32[3,12,1]{1,2,0:T(1,128)}, u32[]{:S(2)}) copy-start(s32[3,12,1]{1,2,0:T(1,128)} %param.6) | copy-start | bytes 436
  264.8 91.4 %copy-start.3 = (s32[3,12,1]{1,2,0:T(1,128)S(1)}, s32[3,12,1]{1,2,0:T(1,128)}, u32[]{:S(2)}) copy-start(s32[3,12,1]{1,2,0:T(1,128)} %param.7) | copy-start | bytes 436
  264.8 141.5 %all-gather.4.cloned.1.call-start = ((), (), s32[]{:S(2)}) async-start(), calls=%async_computation.9 | async-start | bytes 1081344 | tf_op jit(solution)/shard_map/all_gather | solution.py:47
  356.1 83.9 %reduce-scatter.13.cloned.1.call-start = ((), (), s32[]{:S(2)}) async-start(), calls=%async_computation.10 | async-start | bytes 294912 | tf_op jit(solution)/shard_map/reduce_scatter | solution.py:54
  409.7 85.2 %all-gather.6.cloned.1.call-start = ((), (), s32[]{:S(2)}) async-start(), calls=%async_computation.11 | async-start | bytes 1081344 | tf_op jit(solution)/shard_map/all_gather | solution.py:47
  441.7 87.2 %reduce-scatter.15.cloned.1.call-start = ((), (), s32[]{:S(2)}) async-start(), calls=%async_computation.12 | async-start | bytes 294912 | tf_op jit(solution)/shard_map/reduce_scatter | solution.py:54
  498.4 85.7 %all-gather.8.cloned.1.call-start = ((), (), s32[]{:S(2)}) async-start(), calls=%async_computation.13 | async-start | bytes 1081344 | tf_op jit(solution)/shard_map/all_gather | solution.py:47
  530.6 87.2 %reduce-scatter.17.cloned.1.call-start = ((), (), s32[]{:S(2)}) async-start(), calls=%async_computation.14 | async-start | bytes 294912 | tf_op jit(solution)/shard_map/reduce_scatter | solution.py:54
Sparse Core Ops, SparseCore 0:
  37.0 88.8 reduce-scatter.6
  150.6 89.4 reduce-scatter.8
  264.9 89.2 reduce-scatter.10
  357.0 49.2 all-gather.3
  409.9 30.1 reduce-scatter.12
  442.4 52.4 all-gather.5
  498.5 30.3 reduce-scatter.14
  531.8 52.1 all-gather.7
  587.6 30.1 reduce-scatter.16
where the time goes:
time: 631 us; the launch traced here: 626 us
  waiting for transfers between devices  515 us (82%)
  blocking collectives  63.5 us (10%)
  local copies, waits for them, and re-layouts  16.5 us (3%)
  matrix products  15.6 us (2%)
  between operations  13.5 us (2%)
    reduce_scatter x3, waiting for transfers between devices, solve_all(): lax.psum_scatter(term(jnp.int32(0), lax.axis_size('col') * rows_dev).asty...  268 us
    all_gather x3, waiting for transfers between devices, solve_all(): lax.all_gather(current.astype(jnp.bfloat16), 'col', axis=0, tiled=True)  157 us
    reduce_scatter x3, waiting for transfers between devices, solve_all(): lax.psum_scatter(column_sums.astype(jnp.bfloat16), 'row', scatter_dimensi...  91 us
    all_gather x3, blocking collectives, solve_all(): lax.all_gather(current.astype(jnp.bfloat16), 'row', axis=0, tiled=True)  63.5 us
  transfers between devices with their start and end apart: 9, of which 9 were waited for; matrix products, arithmetic and copies ran while one was open for 0% of the time, Pallas kernels for 0%

commit v1 on v0

v1 whole, which is shorter than its diff:
```python
import functools

import jax
import jax.numpy as jnp
from jax import lax
from jax.experimental import pallas as pl
from jax.experimental.pallas import tpu as pltpu
from jax.sharding import PartitionSpec as P

MESH = pl.DeviceIdType.MESH
AXES = ("row", "col")


def apply_inverse(inverse, vector, transposed):
    matrix = inverse.reshape(inverse.shape[0], -1, inverse.shape[0])
    if transposed:
        return jnp.einsum("cir,irn->icn", matrix, vector, precision=lax.Precision.HIGHEST)
    return jnp.einsum("cir,icn->irn", matrix, vector, precision=lax.Precision.HIGHEST)


def peer_id(axis, peer):
    return tuple(peer if name == axis else lax.axis_index(name) for name in AXES)


def greet(axis, n, me):
    barrier = pltpu.get_barrier_semaphore()
    for k in range(1, n):
        pl.semaphore_signal(
            barrier, inc=1, device_id=peer_id(axis, lax.rem(me + k, n)), device_id_type=MESH
        )
    pl.semaphore_wait(barrier, n - 1)


def exchange_sum_kernel(axis, n, x_ref, o_ref, held, send_sem, recv_sem):
    me = lax.axis_index(axis)
    greet(axis, n, me)
    copies = []
    for k in range(1, n):
        peer = lax.rem(me + k, n)
        copy = pltpu.make_async_remote_copy(
            src_ref=x_ref.at[peer],
            dst_ref=held.at[k],
            send_sem=send_sem.at[k],
            recv_sem=recv_sem.at[k],
            device_id=peer_id(axis, peer),
            device_id_type=MESH,
        )
        copy.start()
        copies.append(copy)
    total = x_ref[me].astype(jnp.float32)
    for k in range(1, n):
        copies[k - 1].wait()
        total = total + held[k].astype(jnp.float32)
    o_ref[...] = total


def gather_kernel(axis, n, x_ref, o_ref, held, send_sem, recv_sem):
    me = lax.axis_index(axis)
    greet(axis, n, me)
    copies = []
    for k in range(1, n):
        peer = lax.rem(me + k, n)
        copy = pltpu.make_async_remote_copy(
            src_ref=x_ref,
            dst_ref=held.at[k],
            send_sem=send_sem.at[k],
            recv_sem=recv_sem.at[k],
            device_id=peer_id(axis, peer),
            device_id_type=MESH,
        )
        copy.start()
        copies.append(copy)
    o_ref[me] = x_ref[...]
    for k in range(1, n):
        copies[k - 1].wait()
        o_ref[lax.rem(me + n - k, n)] = held[k]


def exchange_sum(x, axis, n, cid):
    piece = x.shape[1:]
    return pl.pallas_call(
        functools.partial(exchange_sum_kernel, axis, n),
        out_shape=jax.ShapeDtypeStruct(piece, jnp.float32),
        in_specs=[pl.BlockSpec(memory_space=pltpu.VMEM)],
        out_specs=pl.BlockSpec(memory_space=pltpu.VMEM),
        scratch_shapes=[
            pltpu.VMEM((n,) + piece, x.dtype),
            pltpu.SemaphoreType.DMA((n,)),
            pltpu.SemaphoreType.DMA((n,)),
        ],
        compiler_params=pltpu.CompilerParams(collective_id=cid, has_side_effects=True),
    )(x)


def gather(x, axis, n, cid):
    return pl.pallas_call(
        functools.partial(gather_kernel, axis, n),
        out_shape=jax.ShapeDtypeStruct((n,) + x.shape, x.dtype),
        in_specs=[pl.BlockSpec(memory_space=pltpu.VMEM)],
        out_specs=pl.BlockSpec(memory_space=pltpu.VMEM),
        scratch_shapes=[
            pltpu.VMEM((n,) + x.shape, x.dtype),
            pltpu.SemaphoreType.DMA((n,)),
            pltpu.SemaphoreType.DMA((n,)),
        ],
        compiler_params=pltpu.CompilerParams(collective_id=cid, has_side_effects=True),
    )(x)


def solve_all(n_row, n_col, factor_tiles, tile_row, tile_col, right_sides, diag_inverse):
    levels = factor_tiles.shape[0]
    rows_dev = right_sides.shape[1]
    group_rows = rows_dev * n_row
    row_ids = tile_row[:, :, 0]
    col_ids = tile_col[:, :, 0]
    current = apply_inverse(diag_inverse[0], right_sides[0], False)
    solved = [current]
    for section_no in range(1, levels + 1):
        gathered = gather(current.astype(jnp.bfloat16), "row", n_row, 1)
        gathered = gathered.reshape((group_rows,) + current.shape[1:])
        picked = gathered[col_ids[section_no - 1]]
        products = jnp.einsum(
            "tab,tbn->tan", factor_tiles[section_no - 1], picked, preferred_element_type=jnp.float32
        )
        targets = row_ids[section_no - 1]
        places = jnp.arange(n_col * rows_dev, dtype=jnp.int32)
        select = (targets[:, None] == places[None, :]).astype(jnp.float32)
        terms = jnp.einsum("tq,tan->qan", select, products, precision=lax.Precision.HIGHEST)
        terms = terms.astype(jnp.bfloat16).reshape((n_col, rows_dev) + terms.shape[1:])
        row_sums = exchange_sum(terms, "col", n_col, 2)
        current = apply_inverse(diag_inverse[section_no], right_sides[section_no] - row_sums, False)
        solved.append(current)
    current = apply_inverse(diag_inverse[levels], solved[levels], True)
    result = [current]
    columns_here = jnp.arange(group_rows, dtype=jnp.int32)
    for section_no in range(levels - 1, -1, -1):
        everyone = gather(current.astype(jnp.bfloat16), "col", n_col, 3)
        everyone = everyone.reshape((n_col * rows_dev,) + current.shape[1:])
        picked = everyone[row_ids[section_no]]
        spread = jnp.einsum(
            "tab,tan->tbn", factor_tiles[section_no], picked, preferred_element_type=jnp.float32
        )
        select = (col_ids[section_no][:, None] == columns_here[None, :]).astype(jnp.float32)
        column_sums = jnp.einsum("tj,tbn->jbn", select, spread, precision=lax.Precision.HIGHEST)
        column_sums = column_sums.astype(jnp.bfloat16).reshape((n_row, rows_dev) + column_sums.shape[1:])
        received = exchange_sum(column_sums, "row", n_row, 4)
        current = apply_inverse(diag_inverse[section_no], solved[section_no] - received, True)
        result.insert(0, current)
    return jnp.stack(result)


def solution(mesh):
    n_row, n_col = mesh.shape["row"], mesh.shape["col"]
    return jax.shard_map(
        functools.partial(solve_all, n_row, n_col),
        mesh=mesh,
        in_specs=(
            P(None, "row", None, "col"),
            P(None, "row", "col"),
            P(None, "row", "col"),
            P(None, ("col", "row"), None, None),
            P(None, None, ("col", "row")),
        ),
        out_specs=P(None, ("col", "row"), None, None),
        check_vma=False,
    )
```

time: 631 us -> 254 us (0.40)
  waiting for transfers between devices: 515 us -> 0 us
  Pallas kernels: 0 us -> 214 us
  blocking collectives: 63.5 us -> 0 us
  between operations: 13.5 us -> 0.52 us
    reduce_scatter x6 -> x0, waiting for transfers between devices: 359 us -> none  [the longest x3 268 us: solve_all(): lax.psum_scatter(term(jnp.int32(0), lax.axis_size('col') * rows_dev).asty...]
    pallas_call x0 -> x12, Pallas kernels: none -> 214 us  [the longest x6 107 us: exchange_sum(): pl.pallas_call(functools.partial(exchange_sum_kernel, axis, n), out_shape...]
    all_gather x3 -> x0, waiting for transfers between devices: 157 us -> none  [solve_all(): lax.all_gather(current.astype(jnp.bfloat16), 'col', axis=0, tiled=True)]
    all_gather x3 -> x0, blocking collectives: 63.5 us -> none  [solve_all(): lax.all_gather(current.astype(jnp.bfloat16), 'row', axis=0, tiled=True)]
  transfers between devices with their start and end apart: 9 -> 0, of which waited for: 9 -> 0; matrix products, arithmetic and copies ran while one was open for 0% -> 0% of each run, Pallas kernels for 0% -> 0%
where the time goes in v1:
time: 254 us; the launch traced here: 253 us
  Pallas kernels  214 us (84%)
  local copies, waits for them, and re-layouts  18.6 us (7%)
  matrix products  18 us (7%)
    pallas_call x6, Pallas kernels, exchange_sum(): pl.pallas_call(functools.partial(exchange_sum_kernel, axis, n), out_shape...  107 us
    pallas_call x6, Pallas kernels, gather(): pl.pallas_call(functools.partial(gather_kernel, axis, n), out_shape=jax.S...  107 us
    dot_general x4, matrix products, apply_inverse(): jnp.einsum('cir,icn->irn', matrix, vector, precision=lax.Precision.HIGHEST)  6.1 us
    dot_general x4, matrix products, apply_inverse(): jnp.einsum('cir,irn->icn', matrix, vector, precision=lax.Precision.HIGHEST)  5.43 us
    gather x3, local copies, waits for them, and re-layouts, solve_all(): picked = everyone[row_ids[section_no]]  5.43 us

profile of v1, /device:TPU:1, one launch (start us, length us, event | category | flops | bytes accessed | tf_op | source)
XLA Modules:
  0.0 252.9 jit_solution(4048057707227070963)
XLA Ops:
  0.0 0.0 copy-start
  0.0 0.0 copy-start.2
  0.0 0.9 fusion.69
  0.9 0.1 copy.18
  1.0 1.7 fusion.70
  2.6 15.8 %shard_map.55 = bf16[8,2,64,128]{3,2,1,0:T(8,128)(2,1)} custom-call(bf16[2,64,128]{2,1,0:T(8,128)(2,1)} %get-tuple-element.21.x_ref), custom_call_target="tpu_custom_call" | custom-call | tf_op jit(solution)/shard_map/pallas_call | solution.py:96
  18.4 0.7 fusion.65
  19.1 1.5 gather_fusion
  20.7 0.0 copy-done
  20.7 0.2 fusion.22
  20.9 0.0 copy-done.2
  20.9 1.1 convolution_convert_fusion.2
  22.0 1.7 copy.19
  23.7 0.0 copy-start.1
  23.7 23.9 %shard_map.56 = f32[2,64,128]{2,1,0:T(8,128)} custom-call(bf16[32,2,64,128]{3,2,1,0:T(8,128)(2,1)} %bitcast.153), custom_call_target="tpu_custom_call" | custom-call | tf_op jit(solution)/shard_map/pallas_call | solution.py:81
  47.6 0.1 copy.20
  47.7 0.0 copy-done.1
  47.7 1.7 fusion.71
  49.4 12.7 %shard_map.57 = bf16[8,2,64,128]{3,2,1,0:T(8,128)(2,1)} custom-call(bf16[2,64,128]{2,1,0:T(8,128)(2,1)} %get-tuple-element.23.x_ref), custom_call_target="tpu_custom_call" | custom-call | tf_op jit(solution)/shard_map/pallas_call | solution.py:96
  62.1 1.5 gather_fusion.1
  63.6 0.2 fusion.18
  63.8 1.1 convolution_convert_fusion.1
  64.9 1.7 copy.21
  66.6 20.9 %shard_map.58 = f32[2,64,128]{2,1,0:T(8,128)} custom-call(bf16[32,2,64,128]{3,2,1,0:T(8,128)(2,1)} %bitcast.154), custom_call_target="tpu_custom_call" | custom-call | tf_op jit(solution)/shard_map/pallas_call | solution.py:81
  87.5 0.1 copy.22
  87.6 1.7 fusion.72
  89.3 13.1 %shard_map.59 = bf16[8,2,64,128]{3,2,1,0:T(8,128)(2,1)} custom-call(bf16[2,64,128]{2,1,0:T(8,128)(2,1)} %get-tuple-element.25.x_ref), custom_call_target="tpu_custom_call" | custom-call | tf_op jit(solution)/shard_map/pallas_call | solution.py:96
  102.4 1.5 gather_fusion.2
  104.0 0.2 fusion.14
  104.2 1.1 convolution_convert_fusion
  105.3 1.7 copy.23
  106.9 22.2 %shard_map.60 = f32[2,64,128]{2,1,0:T(8,128)} custom-call(bf16[32,2,64,128]{3,2,1,0:T(8,128)(2,1)} %bitcast.155), custom_call_target="tpu_custom_call" | custom-call | tf_op jit(solution)/shard_map/pallas_call | solution.py:81
  129.1 0.1 reshape_squeeze.19
  129.2 1.1 fusion.30
  130.3 0.8 bitcast_convert_fusion.2
  131.2 0.0 copy-start.3
  131.2 21.4 %shard_map.61 = bf16[32,2,64,128]{3,2,1,0:T(8,128)(2,1)} custom-call(bf16[2,64,128]{2,1,0:T(8,128)(2,1)} %get-tuple-element.27.x_ref), custom_call_target="tpu_custom_call" | custom-call | tf_op jit(solution)/shard_map/pallas_call | solution.py:96
  152.6 1.8 gather_fusion.3
  154.4 0.3 fusion.12
  154.7 0.0 copy-done.3
  154.7 0.6 convolution_convert_fusion.5
  155.3 0.8 copy.25
  156.1 13.4 %shard_map.62 = f32[2,64,128]{2,1,0:T(8,128)} custom-call(bf16[8,2,64,128]{3,2,1,0:T(8,128)(2,1)} %bitcast.159), custom_call_target="tpu_custom_call" | custom-call | tf_op jit(solution)/shard_map/pallas_call | solution.py:81
  169.5 1.7 bitcast_convert_fusion.1
  171.3 22.0 %shard_map.63 = bf16[32,2,64,128]{3,2,1,0:T(8,128)(2,1)} custom-call(bf16[2,64,128]{2,1,0:T(8,128)(2,1)} %get-tuple-element.29.x_ref), custom_call_target="tpu_custom_call" | custom-call | tf_op jit(solution)/shard_map/pallas_call | solution.py:96
  193.3 1.8 gather_fusion.4
  195.3 0.3 fusion.16
  195.6 0.6 convolution_convert_fusion.4
  196.2 0.8 copy.27
  197.0 13.4 %shard_map.64 = f32[2,64,128]{2,1,0:T(8,128)} custom-call(bf16[8,2,64,128]{3,2,1,0:T(8,128)(2,1)} %bitcast.160), custom_call_target="tpu_custom_call" | custom-call | tf_op jit(solution)/shard_map/pallas_call | solution.py:81
  210.4 1.7 bitcast_convert_fusion
  212.1 22.0 %shard_map.65 = bf16[32,2,64,128]{3,2,1,0:T(8,128)(2,1)} custom-call(bf16[2,64,128]{2,1,0:T(8,128)(2,1)} %get-tuple-element.31.x_ref), custom_call_target="tpu_custom_call" | custom-call | tf_op jit(solution)/shard_map/pallas_call | solution.py:96
  234.2 1.8 gather_fusion.5
  236.0 0.3 fusion.20
  236.2 0.6 convolution_convert_fusion.3
  236.8 0.8 copy.29
  237.6 13.4 %shard_map.66 = f32[2,64,128]{2,1,0:T(8,128)} custom-call(bf16[8,2,64,128]{3,2,1,0:T(8,128)(2,1)} %bitcast.161), custom_call_target="tpu_custom_call" | custom-call | tf_op jit(solution)/shard_map/pallas_call | solution.py:81
  251.1 1.1 convolution_bitcast_fusion
  252.2 0.7 pad_maximum_fusion
  (7 shorter events, 0.0 us)
Async XLA Ops:
  0.0 20.7 %copy-start = (bf16[3,12,64,64]{3,2,1,0:T(8,128)(2,1)S(1)}, bf16[3,12,64,64]{3,2,1,0:T(8,128)(2,1)}, u32[]{:S(2)}) copy-start(bf16[3,12,64,64]{3,2,1,0:T(8,128)(2,1)} %param.5) | copy-start | bytes 884740
  0.0 20.9 %copy-start.2 = (s32[3,12,1]{1,2,0:T(1,128)S(1)}, s32[3,12,1]{1,2,0:T(1,128)}, u32[]{:S(2)}) copy-start(s32[3,12,1]{1,2,0:T(1,128)} %param.6) | copy-start | bytes 436
  23.7 24.0 %copy-start.1 = (f32[4,2,64,128]{3,2,1,0:T(8,128)S(1)}, f32[4,2,64,128]{3,2,1,0:T(8,128)}, u32[]{:S(2)}) copy-start(f32[4,2,64,128]{3,2,1,0:T(8,128)} %param.8) | copy-start | bytes 786436
  131.2 23.5 %copy-start.3 = (s32[3,12,1]{1,2,0:T(1,128)S(1)}, s32[3,12,1]{1,2,0:T(1,128)}, u32[]{:S(2)}) copy-start(s32[3,12,1]{1,2,0:T(1,128)} %param.7) | copy-start | bytes 436

commit v2 on v0

v2 whole, which is shorter than its diff:
```python
import functools

import jax
import jax.numpy as jnp
from jax import lax
from jax.experimental import pallas as pl
from jax.experimental.pallas import tpu as pltpu
from jax.sharding import PartitionSpec as P

MESH = pl.DeviceIdType.MESH
AXES = ("row", "col")
HIGHEST = lax.Precision.HIGHEST


def peer_id(axis, peer):
    return tuple(peer if name == axis else lax.axis_index(name) for name in AXES)


def level_kernel(ex, ga, applies, *refs):
    refs = list(refs)
    x_ref = refs.pop(0) if ex else None
    base_ref = refs.pop(0)
    g_refs = [refs.pop(0) for _ in applies]
    out_ref = refs.pop(0)
    gathered_ref = refs.pop(0) if ga else None
    if ex:
        held_x, ex_send, ex_recv = refs.pop(0), refs.pop(0), refs.pop(0)
    if ga:
        held_g, stage, ga_send, ga_recv = refs.pop(0), refs.pop(0), refs.pop(0), refs.pop(0)

    groups = [g for g in (ex, ga) if g]
    barrier = pltpu.get_barrier_semaphore()
    for axis, n in groups:
        me = lax.axis_index(axis)
        for k in range(1, n):
            pl.semaphore_signal(
                barrier, inc=1, device_id=peer_id(axis, lax.rem(me + k, n)), device_id_type=MESH
            )
    pl.semaphore_wait(barrier, sum(n - 1 for _, n in groups))

    value = base_ref[...]
    if ex:
        axis, n = ex
        me = lax.axis_index(axis)
        copies = []
        for k in range(1, n):
            peer = lax.rem(me + k, n)
            copy = pltpu.make_async_remote_copy(
                src_ref=x_ref.at[peer],
                dst_ref=held_x.at[k],
                send_sem=ex_send.at[k],
                recv_sem=ex_recv.at[k],
                device_id=peer_id(axis, peer),
                device_id_type=MESH,
            )
            copy.start()
            copies.append(copy)
        total = x_ref[me].astype(jnp.float32)
        for k in range(1, n):
            copies[k - 1].wait()
            total = total + held_x[k].astype(jnp.float32)
        value = value - total
    for g_ref in g_refs:
        value = jnp.stack(
            [
                jnp.dot(g_ref[i], value[i], precision=HIGHEST, preferred_element_type=jnp.float32)
                for i in range(value.shape[0])
            ]
        )
    out_ref[...] = value
    if ga:
        axis, n = ga
        me = lax.axis_index(axis)
        stage[...] = value.astype(stage.dtype)
        copies = []
        for k in range(1, n):
            peer = lax.rem(me + k, n)
            copy = pltpu.make_async_remote_copy(
                src_ref=stage,
                dst_ref=held_g.at[k],
                send_sem=ga_send.at[k],
                recv_sem=ga_recv.at[k],
                device_id=peer_id(axis, peer),
                device_id_type=MESH,
            )
            copy.start()
            copies.append(copy)
        gathered_ref[me] = value.astype(gathered_ref.dtype)
        for k in range(1, n):
            copies[k - 1].wait()
            gathered_ref[lax.rem(me + n - k, n)] = held_g[k]


def level(cid, x, base, gs, ex=None, ga=None):
    piece = base.shape
    vmem = pl.BlockSpec(memory_space=pltpu.VMEM)
    args = ([x] if ex else []) + [base] + list(gs)
    out_shape = [jax.ShapeDtypeStruct(piece, jnp.float32)]
    scratch = []
    if ex:
        scratch += [
            pltpu.VMEM((ex[1],) + piece, jnp.bfloat16),
            pltpu.SemaphoreType.DMA((ex[1],)),
            pltpu.SemaphoreType.DMA((ex[1],)),
        ]
    if ga:
        out_shape.append(jax.ShapeDtypeStruct((ga[1],) + piece, jnp.bfloat16))
        scratch += [
            pltpu.VMEM((ga[1],) + piece, jnp.bfloat16),
            pltpu.VMEM(piece, jnp.bfloat16),
            pltpu.SemaphoreType.DMA((ga[1],)),
            pltpu.SemaphoreType.DMA((ga[1],)),
        ]
    outs = pl.pallas_call(
        functools.partial(level_kernel, ex, ga, tuple(range(len(gs)))),
        out_shape=out_shape,
        in_specs=[vmem] * len(args),
        out_specs=[vmem] * len(out_shape),
        scratch_shapes=scratch,
        compiler_params=pltpu.CompilerParams(collective_id=cid, has_side_effects=True),
    )(*args)
    return outs if ga else (outs[0], None)


def solve_all(n_row, n_col, factor_tiles, tile_row, tile_col, right_sides, diag_inverse):
    levels = factor_tiles.shape[0]
    rows_dev = right_sides.shape[1]
    block = right_sides.shape[2]
    group_rows = rows_dev * n_row
    row_ids = tile_row[:, :, 0]
    col_ids = tile_col[:, :, 0]
    split = diag_inverse.reshape(levels + 1, block, rows_dev, block)
    g_fwd = split.transpose(0, 2, 3, 1)
    g_bwd = split.transpose(0, 2, 1, 3)
    row_axis, col_axis = ("row", n_row), ("col", n_col)

    current, gathered = level(1, None, right_sides[0], [g_fwd[0]], ga=row_axis)
    solved = [current]
    for section_no in range(1, levels + 1):
        picked = gathered.reshape((group_rows,) + current.shape[1:])[col_ids[section_no - 1]]
        products = jnp.einsum(
            "tab,tbn->tan", factor_tiles[section_no - 1], picked, preferred_element_type=jnp.float32
        )
        targets = row_ids[section_no - 1]
        places = jnp.arange(n_col * rows_dev, dtype=jnp.int32)
        select = (targets[:, None] == places[None, :]).astype(jnp.float32)
        terms = jnp.einsum("tq,tan->qan", select, products, precision=HIGHEST)
        terms = terms.astype(jnp.bfloat16).reshape((n_col, rows_dev) + terms.shape[1:])
        if section_no < levels:
            current, gathered = level(2, terms, right_sides[section_no], [g_fwd[section_no]],
                                      ex=col_axis, ga=row_axis)
            solved.append(current)
        else:
            current, gathered = level(3, terms, right_sides[section_no],
                                      [g_fwd[section_no], g_bwd[section_no]], ex=col_axis, ga=col_axis)
    result = [current]
    columns_here = jnp.arange(group_rows, dtype=jnp.int32)
    for section_no in range(levels - 1, -1, -1):
        picked = gathered.reshape((n_col * rows_dev,) + current.shape[1:])[row_ids[section_no]]
        spread = jnp.einsum(
            "tab,tan->tbn", factor_tiles[section_no], picked, preferred_element_type=jnp.float32
        )
        select = (col_ids[section_no][:, None] == columns_here[None, :]).astype(jnp.float32)
        column_sums = jnp.einsum("tj,tbn->jbn", select, spread, precision=HIGHEST)
        column_sums = column_sums.astype(jnp.bfloat16).reshape((n_row, rows_dev) + column_sums.shape[1:])
        if section_no > 0:
            current, gathered = level(4, column_sums, solved[section_no], [g_bwd[section_no]],
                                      ex=row_axis, ga=col_axis)
        else:
            current, _ = level(5, column_sums, solved[section_no], [g_bwd[section_no]], ex=row_axis)
        result.insert(0, current)
    return jnp.stack(result)


def solution(mesh):
    n_row, n_col = mesh.shape["row"], mesh.shape["col"]
    return jax.shard_map(
        functools.partial(solve_all, n_row, n_col),
        mesh=mesh,
        in_specs=(
            P(None, "row", None, "col"),
            P(None, "row", "col"),
            P(None, "row", "col"),
            P(None, ("col", "row"), None, None),
            P(None, None, ("col", "row")),
        ),
        out_specs=P(None, ("col", "row"), None, None),
        check_vma=False,
    )
```

time: 631 us -> 223 us (0.35)
  waiting for transfers between devices: 515 us -> 0 us
  Pallas kernels: 0 us -> 194 us
  blocking collectives: 63.5 us -> 0 us
  between operations: 13.5 us -> 0.37 us
  matrix products: 15.6 us -> 6.59 us
    reduce_scatter x6 -> x0, waiting for transfers between devices: 359 us -> none  [the longest x3 268 us: solve_all(): lax.psum_scatter(term(jnp.int32(0), lax.axis_size('col') * rows_dev).asty...]
    pallas_call x0 -> x7, Pallas kernels: none -> 194 us  [level(): pl.pallas_call(functools.partial(level_kernel, ex, ga, tuple(range(len(gs...]
    all_gather x3 -> x0, waiting for transfers between devices: 157 us -> none  [solve_all(): lax.all_gather(current.astype(jnp.bfloat16), 'col', axis=0, tiled=True)]
    all_gather x3 -> x0, blocking collectives: 63.5 us -> none  [solve_all(): lax.all_gather(current.astype(jnp.bfloat16), 'row', axis=0, tiled=True)]
    dot_general x14 -> x6, matrix products: 14.3 us -> 5.28 us  [the longest x3 3.32 us: solve_all(): terms = jnp.einsum('tq,tan->qan', select, products, precision=HIGHEST)]
  transfers between devices with their start and end apart: 9 -> 0, of which waited for: 9 -> 0; matrix products, arithmetic and copies ran while one was open for 0% -> 0% of each run, Pallas kernels for 0% -> 0%
where the time goes in v2:
time: 223 us
  Pallas kernels  194 us (87%)
  local copies, waits for them, and re-layouts  20.1 us (9%)
  matrix products  6.59 us (3%)
    pallas_call x7, Pallas kernels, level(): pl.pallas_call(functools.partial(level_kernel, ex, ga, tuple(range(len(gs...  194 us
    gather x3, local copies, waits for them, and re-layouts, solve_all(): gathered.reshape((n_col * rows_dev,) + current.shape[1:])  5.43 us
    convert_element_type x3, local copies, waits for them, and re-layouts, solve_all(): terms.astype(jnp.bfloat16).reshape((n_col, rows_dev) + terms.shape[1:])  5.01 us
    gather x3, local copies, waits for them, and re-layouts, solve_all(): gathered.reshape((group_rows,) + current.shape[1:])[col_ids[section_no - 1]]  4.6 us

profile of v2, /device:TPU:1, one launch (start us, length us, event | category | flops | bytes accessed | tf_op | source)
XLA Modules:
  0.0 222.7 jit_solution(310076233883842389)
XLA Ops:
  0.0 1.1 reshape.231
  1.1 0.0 copy-start.1
  1.1 0.1 copy.16
  1.2 0.0 copy-start.6
  1.3 0.0 copy-start
  1.3 0.8 slice_bitcast_fusion
  2.1 0.0 copy-start.5
  2.1 0.0 copy-done.1
  2.1 0.7 slice_bitcast_fusion.8
  2.8 16.1 %shard_map.55 = (f32[2,64,128]{2,1,0:T(8,128)}, bf16[8,2,64,128]{3,2,1,0:T(8,128)(2,1)}) custom-call(f32[2,64,128]{2,1,0:T(8,128)} %get-tuple-element.39.refs_0_, f32[2,64,64]{2,1,0:T(8,128)} %get-tuple-element.55.refs_1_), custom_call_target="tpu_custom_call" | custom-call | tf_op jit(solution)/shard_map/pallas_call | solution.py:114
  18.9 0.0 copy-done.6
  19.0 1.5 gather_fusion
  20.5 0.0 copy-done
  20.5 0.2 fusion.22
  20.7 0.0 copy-done.5
  20.7 1.1 convolution_convert_fusion.2
  21.9 1.7 copy.17
  23.5 34.0 %shard_map.56 = (f32[2,64,128]{2,1,0:T(8,128)}, bf16[8,2,64,128]{3,2,1,0:T(8,128)(2,1)}) custom-call(bf16[32,2,64,128]{3,2,1,0:T(8,128)(2,1)} %bitcast.138, f32[2,64,128]{2,1,0:T(8,128)} %get-tuple-element.38.refs_1_, f32[2,64,64]{2,1,0:T(8,128)} %get-tuple-element.56.refs_2_), custom_call_target="tpu_custom_call" | custom-call | tf_op jit(solution)/shard_map/pallas_call | solution.py:114
  57.5 1.5 gather_fusion.1
  59.1 0.2 fusion.18
  59.3 1.1 convolution_convert_fusion.1
  60.4 1.7 copy.18
  62.0 30.2 %shard_map.57 = (f32[2,64,128]{2,1,0:T(8,128)}, bf16[8,2,64,128]{3,2,1,0:T(8,128)(2,1)}) custom-call(bf16[32,2,64,128]{3,2,1,0:T(8,128)(2,1)} %bitcast.139, f32[2,64,128]{2,1,0:T(8,128)} %get-tuple-element.40.refs_1_, f32[2,64,64]{2,1,0:T(8,128)} %get-tuple-element.57.refs_2_), custom_call_target="tpu_custom_call" | custom-call | tf_op jit(solution)/shard_map/pallas_call | solution.py:114
  92.2 1.5 gather_fusion.2
  93.8 0.2 fusion.14
  94.0 1.1 convolution_convert_fusion
  95.1 1.7 copy.19
  96.8 39.5 %shard_map.58 = (f32[2,64,128]{2,1,0:T(8,128)}, bf16[32,2,64,128]{3,2,1,0:T(8,128)(2,1)}) custom-call(bf16[32,2,64,128]{3,2,1,0:T(8,128)(2,1)} %bitcast.137, f32[2,64,128]{2,1,0:T(8,128)} %get-tuple-element.37.refs_1_, f32[2,64,64]{2,1,0:T(8,128)} %get-tuple-element.58.refs_2_, f32[2,64,64]{2,1,0:T(8,128)} %get-tuple-element.32.refs_3_), custom_call_target="tpu_custom_call" | custom-call | tf_op jit(solution)/shard_map/pallas_call | solution.py:114
  136.3 1.8 gather_fusion.3
  138.1 0.3 fusion.12
  138.4 0.6 convolution_convert_fusion.5
  139.0 0.8 copy.21
  139.7 29.2 %shard_map.59 = (f32[2,64,128]{2,1,0:T(8,128)}, bf16[32,2,64,128]{3,2,1,0:T(8,128)(2,1)}) custom-call(bf16[8,2,64,128]{3,2,1,0:T(8,128)(2,1)} %bitcast.141, f32[2,64,128]{2,1,0:T(8,128)} %get-tuple-element.21.refs_1_, f32[2,64,64]{2,1,0:T(8,128)} %get-tuple-element.31.refs_2_), custom_call_target="tpu_custom_call" | custom-call | tf_op jit(solution)/shard_map/pallas_call | solution.py:114
  169.0 1.8 gather_fusion.4
  170.8 0.3 fusion.16
  171.0 0.8 convolution_convert_fusion.4
  171.8 0.8 copy.22
  172.6 31.1 %shard_map.60 = (f32[2,64,128]{2,1,0:T(8,128)}, bf16[32,2,64,128]{3,2,1,0:T(8,128)(2,1)}) custom-call(bf16[8,2,64,128]{3,2,1,0:T(8,128)(2,1)} %bitcast.142, f32[2,64,128]{2,1,0:T(8,128)} %get-tuple-element.23.refs_1_, f32[2,64,64]{2,1,0:T(8,128)} %get-tuple-element.30.refs_2_), custom_call_target="tpu_custom_call" | custom-call | tf_op jit(solution)/shard_map/pallas_call | solution.py:114
  203.7 1.8 gather_fusion.5
  205.5 0.3 fusion.20
  205.8 0.0 copy-start.2
  205.8 0.0 copy-start.3
  205.8 0.0 copy-start.4
  205.8 0.6 convolution_convert_fusion.3
  206.4 0.8 copy.23
  207.2 13.9 %shard_map.61 = f32[2,64,128]{2,1,0:T(8,128)} custom-call(bf16[8,2,64,128]{3,2,1,0:T(8,128)(2,1)} %bitcast.140, f32[2,64,128]{2,1,0:T(8,128)} %get-tuple-element.25.refs_1_, f32[2,64,64]{2,1,0:T(8,128)} %get-tuple-element.29.refs_2_), custom_call_target="tpu_custom_call" | custom-call | tf_op jit(solution)/shard_map/pallas_call | solution.py:114
  221.1 0.0 copy-done.2
  221.1 0.0 copy-done.3
  221.1 0.0 copy-done.4
  221.1 1.6 pad_maximum_fusion
  (9 shorter events, 0.1 us)
Async XLA Ops:
  1.1 1.0 copy-start.1
  1.2 17.7 %copy-start.6 = (s32[3,12,1]{1,2,0:T(1,128)S(1)}, s32[3,12,1]{1,2,0:T(1,128)}, u32[]{:S(2)}) copy-start(s32[3,12,1]{1,2,0:T(1,128)} %param.7) | copy-start | bytes 436
  1.3 19.2 %copy-start = (bf16[3,12,64,64]{3,2,1,0:T(8,128)(2,1)S(1)}, bf16[3,12,64,64]{3,2,1,0:T(8,128)(2,1)}, u32[]{:S(2)}) copy-start(bf16[3,12,64,64]{3,2,1,0:T(8,128)(2,1)} %param.5) | copy-start | bytes 884740
  2.1 18.6 %copy-start.5 = (s32[3,12,1]{1,2,0:T(1,128)S(1)}, s32[3,12,1]{1,2,0:T(1,128)}, u32[]{:S(2)}) copy-start(s32[3,12,1]{1,2,0:T(1,128)} %param.6) | copy-start | bytes 436
  205.8 15.4 %copy-start.2 = (f32[2,64,128]{2,1,0:T(8,128)S(1)}, f32[2,64,128]{2,1,0:T(8,128)}, u32[]{:S(2)}) copy-start(f32[2,64,128]{2,1,0:T(8,128)} %get-tuple-element.28) | copy-start | bytes 196612
  205.8 15.4 %copy-start.3 = (f32[2,64,128]{2,1,0:T(8,128)S(1)}, f32[2,64,128]{2,1,0:T(8,128)}, u32[]{:S(2)}) copy-start(f32[2,64,128]{2,1,0:T(8,128)} %get-tuple-element.27) | copy-start | bytes 196612
  205.8 15.4 %copy-start.4 = (f32[2,64,128]{2,1,0:T(8,128)S(1)}, f32[2,64,128]{2,1,0:T(8,128)}, u32[]{:S(2)}) copy-start(f32[2,64,128]{2,1,0:T(8,128)} %get-tuple-element.26) | copy-start | bytes 196612

commit v3 on v2

--- a/solution.py
+++ b/solution.py
@@ -27,6 +27,7 @@
         held_x, ex_send, ex_recv = refs.pop(0), refs.pop(0), refs.pop(0)
     if ga:
         held_g, stage, ga_send, ga_recv = refs.pop(0), refs.pop(0), refs.pop(0), refs.pop(0)
+    blocks = base_ref.shape[0]
 
     groups = [g for g in (ex, ga) if g]
     barrier = pltpu.get_barrier_semaphore()
@@ -38,57 +39,70 @@
             )
     pl.semaphore_wait(barrier, sum(n - 1 for _, n in groups))
 
-    value = base_ref[...]
-    if ex:
+    def exchange_copies(kb):
         axis, n = ex
         me = lax.axis_index(axis)
         copies = []
         for k in range(1, n):
             peer = lax.rem(me + k, n)
             copy = pltpu.make_async_remote_copy(
-                src_ref=x_ref.at[peer],
-                dst_ref=held_x.at[k],
-                send_sem=ex_send.at[k],
-                recv_sem=ex_recv.at[k],
+                src_ref=x_ref.at[peer, kb],
+                dst_ref=held_x.at[k, kb],
+                send_sem=ex_send.at[kb, k],
+                recv_sem=ex_recv.at[kb, k],
                 device_id=peer_id(axis, peer),
                 device_id_type=MESH,
             )
             copy.start()
             copies.append(copy)
-        total = x_ref[me].astype(jnp.float32)
-        for k in range(1, n):
-            copies[k - 1].wait()
-            total = total + held_x[k].astype(jnp.float32)
-        value = value - total
-    for g_ref in g_refs:
-        value = jnp.stack(
-            [
-                jnp.dot(g_ref[i], value[i], precision=HIGHEST, preferred_element_type=jnp.float32)
-                for i in range(value.shape[0])
-            ]
-        )
-    out_ref[...] = value
+        return copies
+
+    gather_copies = []
+    pending = exchange_copies(0) if ex else None
+    for kb in range(blocks):
+        value = base_ref[kb]
+        if ex:
+            axis, n = ex
+            me = lax.axis_index(axis)
+            copies = pending
+            if kb + 1 < blocks:
+                for copy in copies:
+                    copy.wait_send()
+                pending = exchange_copies(kb + 1)
+            total = x_ref[me, kb].astype(jnp.float32)
+            for k in range(1, n):
+                copies[k - 1].wait_recv()
+                total = total + held_x[k, kb].astype(jnp.float32)
+            if kb + 1 == blocks:
+                for copy in copies:
+                    copy.wait_send()
+            value = value - total
+        for g_ref in g_refs:
+            value = jnp.dot(g_ref[kb], value, precision=HIGHEST, preferred_element_type=jnp.float32)
+        out_ref[kb] = value
+        if ga:
+            axis, n = ga
+            me = lax.axis_index(axis)
+            stage[kb] = value.astype(stage.dtype)
+            for k in range(1, n):
+                peer = lax.rem(me + k, n)
+                copy = pltpu.make_async_remote_copy(
+                    src_ref=stage.at[kb],
+                    dst_ref=held_g.at[k, kb],
+                    send_sem=ga_send.at[kb, k],
+                    recv_sem=ga_recv.at[kb, k],
+                    device_id=peer_id(axis, peer),
+                    device_id_type=MESH,
+                )
+                copy.start()
+                gather_copies.append((kb, k, copy))
+            gathered_ref[me, kb] = value.astype(gathered_ref.dtype)
     if ga:
         axis, n = ga
         me = lax.axis_index(axis)
-        stage[...] = value.astype(stage.dtype)
-        copies = []
-        for k in range(1, n):
-            peer = lax.rem(me + k, n)
-            copy = pltpu.make_async_remote_copy(
-                src_ref=stage,
-                dst_ref=held_g.at[k],
-                send_sem=ga_send.at[k],
-                recv_sem=ga_recv.at[k],
-                device_id=peer_id(axis, peer),
-                device_id_type=MESH,
-            )
-            copy.start()
-            copies.append(copy)
-        gathered_ref[me] = value.astype(gathered_ref.dtype)
-        for k in range(1, n):
-            copies[k - 1].wait()
-            gathered_ref[lax.rem(me + n - k, n)] = held_g[k]
+        for kb, k, copy in gather_copies:
+            copy.wait()
+            gathered_ref[lax.rem(me + n - k, n), kb] = held_g[k, kb]
 
 
 def level(cid, x, base, gs, ex=None, ga=None):
@@ -100,16 +114,16 @@
     if ex:
         scratch += [
             pltpu.VMEM((ex[1],) + piece, jnp.bfloat16),
-            pltpu.SemaphoreType.DMA((ex[1],)),
-            pltpu.SemaphoreType.DMA((ex[1],)),
+            pltpu.SemaphoreType.DMA((piece[0], ex[1])),
+            pltpu.SemaphoreType.DMA((piece[0], ex[1])),
         ]
     if ga:
         out_shape.append(jax.ShapeDtypeStruct((ga[1],) + piece, jnp.bfloat16))
         scratch += [
             pltpu.VMEM((ga[1],) + piece, jnp.bfloat16),
             pltpu.VMEM(piece, jnp.bfloat16),
-            pltpu.SemaphoreType.DMA((ga[1],)),
-            pltpu.SemaphoreType.DMA((ga[1],)),
+            pltpu.SemaphoreType.DMA((piece[0], ga[1])),
+            pltpu.SemaphoreType.DMA((piece[0], ga[1])),
         ]
     outs = pl.pallas_call(
         functools.partial(level_kernel, ex, ga, tuple(range(len(gs)))),

time: 223 us -> 209 us (0.937)
  Pallas kernels: 194 us -> 179 us
    pallas_call x7, Pallas kernels: 194 us -> 179 us  [level(): pl.pallas_call(functools.partial(level_kernel, ex, ga, tuple(range(len(gs...]
where the time goes in v3:
time: 209 us; the launch traced here: 208 us
  Pallas kernels  179 us (86%)
  local copies, waits for them, and re-layouts  20.3 us (10%)
  matrix products  6.41 us (3%)
    pallas_call x7, Pallas kernels, level(): pl.pallas_call(functools.partial(level_kernel, ex, ga, tuple(range(len(gs...  179 us
    gather x3, local copies, waits for them, and re-layouts, solve_all(): gathered.reshape((n_col * rows_dev,) + current.shape[1:])  5.43 us
    convert_element_type x3, local copies, waits for them, and re-layouts, solve_all(): terms.astype(jnp.bfloat16).reshape((n_col, rows_dev) + terms.shape[1:])  5.01 us
    gather x3, local copies, waits for them, and re-layouts, solve_all(): gathered.reshape((group_rows,) + current.shape[1:])[col_ids[section_no - 1]]  4.6 us

profile of v3, /device:TPU:1, one launch (start us, length us, event | category | flops | bytes accessed | tf_op | source)
XLA Modules:
  0.0 208.1 jit_solution(11354374344818218095)
XLA Ops:
  0.0 1.1 reshape.231
  1.1 0.0 copy-start.1
  1.1 0.1 copy.16
  1.2 0.0 copy-start.6
  1.3 0.0 copy-start
  1.3 0.8 slice_bitcast_fusion
  2.1 0.0 copy-start.5
  2.1 0.0 copy-done.1
  2.1 0.7 slice_bitcast_fusion.8
  2.8 16.2 %shard_map.55 = (f32[2,64,128]{2,1,0:T(8,128)}, bf16[8,2,64,128]{3,2,1,0:T(8,128)(2,1)}) custom-call(f32[2,64,128]{2,1,0:T(8,128)} %get-tuple-element.39.refs_0_, f32[2,64,64]{2,1,0:T(8,128)} %get-tuple-element.55.refs_1_), custom_call_target="tpu_custom_call" | custom-call | tf_op jit(solution)/shard_map/pallas_call | solution.py:128
  19.0 0.0 copy-done.6
  19.1 1.5 gather_fusion
  20.6 0.0 copy-done
  20.6 0.2 fusion.22
  20.8 0.0 copy-done.5
  20.8 1.1 convolution_convert_fusion.2
  21.9 1.7 copy.17
  23.6 31.4 %shard_map.56 = (f32[2,64,128]{2,1,0:T(8,128)}, bf16[8,2,64,128]{3,2,1,0:T(8,128)(2,1)}) custom-call(bf16[32,2,64,128]{3,2,1,0:T(8,128)(2,1)} %bitcast.138, f32[2,64,128]{2,1,0:T(8,128)} %get-tuple-element.38.refs_1_, f32[2,64,64]{2,1,0:T(8,128)} %get-tuple-element.56.refs_2_), custom_call_target="tpu_custom_call" | custom-call | tf_op jit(solution)/shard_map/pallas_call | solution.py:128
  55.0 1.5 gather_fusion.1
  56.5 0.2 fusion.18
  56.7 1.1 convolution_convert_fusion.1
  57.9 1.7 copy.18
  59.5 26.4 %shard_map.57 = (f32[2,64,128]{2,1,0:T(8,128)}, bf16[8,2,64,128]{3,2,1,0:T(8,128)(2,1)}) custom-call(bf16[32,2,64,128]{3,2,1,0:T(8,128)(2,1)} %bitcast.139, f32[2,64,128]{2,1,0:T(8,128)} %get-tuple-element.40.refs_1_, f32[2,64,64]{2,1,0:T(8,128)} %get-tuple-element.57.refs_2_), custom_call_target="tpu_custom_call" | custom-call | tf_op jit(solution)/shard_map/pallas_call | solution.py:128
  85.9 1.5 gather_fusion.2
  87.4 0.2 fusion.14
  87.6 1.1 convolution_convert_fusion
  88.7 1.7 copy.19
  90.4 35.1 %shard_map.58 = (f32[2,64,128]{2,1,0:T(8,128)}, bf16[32,2,64,128]{3,2,1,0:T(8,128)(2,1)}) custom-call(bf16[32,2,64,128]{3,2,1,0:T(8,128)(2,1)} %bitcast.137, f32[2,64,128]{2,1,0:T(8,128)} %get-tuple-element.37.refs_1_, f32[2,64,64]{2,1,0:T(8,128)} %get-tuple-element.58.refs_2_, f32[2,64,64]{2,1,0:T(8,128)} %get-tuple-element.32.refs_3_), custom_call_target="tpu_custom_call" | custom-call | tf_op jit(solution)/shard_map/pallas_call | solution.py:128
  125.6 1.8 gather_fusion.3
  127.4 0.3 fusion.12
  127.7 0.6 convolution_convert_fusion.5
  128.3 1.0 copy.21
  129.2 29.8 %shard_map.59 = (f32[2,64,128]{2,1,0:T(8,128)}, bf16[32,2,64,128]{3,2,1,0:T(8,128)(2,1)}) custom-call(bf16[8,2,64,128]{3,2,1,0:T(8,128)(2,1)} %bitcast.141, f32[2,64,128]{2,1,0:T(8,128)} %get-tuple-element.21.refs_1_, f32[2,64,64]{2,1,0:T(8,128)} %get-tuple-element.31.refs_2_), custom_call_target="tpu_custom_call" | custom-call | tf_op jit(solution)/shard_map/pallas_call | solution.py:128
  159.0 1.8 gather_fusion.4
  160.8 0.3 fusion.16
  161.1 0.6 convolution_convert_fusion.4
  161.7 0.8 copy.22
  162.5 27.0 %shard_map.60 = (f32[2,64,128]{2,1,0:T(8,128)}, bf16[32,2,64,128]{3,2,1,0:T(8,128)(2,1)}) custom-call(bf16[8,2,64,128]{3,2,1,0:T(8,128)(2,1)} %bitcast.142, f32[2,64,128]{2,1,0:T(8,128)} %get-tuple-element.23.refs_1_, f32[2,64,64]{2,1,0:T(8,128)} %get-tuple-element.30.refs_2_), custom_call_target="tpu_custom_call" | custom-call | tf_op jit(solution)/shard_map/pallas_call | solution.py:128
  189.5 1.8 gather_fusion.5
  191.3 0.3 fusion.20
  191.6 0.0 copy-start.2
  191.6 0.0 copy-start.3
  191.6 0.0 copy-start.4
  191.6 0.6 convolution_convert_fusion.3
  192.2 0.8 copy.23
  193.0 13.5 %shard_map.61 = f32[2,64,128]{2,1,0:T(8,128)} custom-call(bf16[8,2,64,128]{3,2,1,0:T(8,128)(2,1)} %bitcast.140, f32[2,64,128]{2,1,0:T(8,128)} %get-tuple-element.25.refs_1_, f32[2,64,64]{2,1,0:T(8,128)} %get-tuple-element.29.refs_2_), custom_call_target="tpu_custom_call" | custom-call | tf_op jit(solution)/shard_map/pallas_call | solution.py:128
  206.5 0.0 copy-done.2
  206.5 0.0 copy-done.3
  206.5 0.0 copy-done.4
  206.5 1.6 pad_maximum_fusion
  (9 shorter events, 0.1 us)
Async XLA Ops:
  1.1 1.0 copy-start.1
  1.2 17.8 %copy-start.6 = (s32[3,12,1]{1,2,0:T(1,128)S(1)}, s32[3,12,1]{1,2,0:T(1,128)}, u32[]{:S(2)}) copy-start(s32[3,12,1]{1,2,0:T(1,128)} %param.7) | copy-start | bytes 436
  1.3 19.3 %copy-start = (bf16[3,12,64,64]{3,2,1,0:T(8,128)(2,1)S(1)}, bf16[3,12,64,64]{3,2,1,0:T(8,128)(2,1)}, u32[]{:S(2)}) copy-start(bf16[3,12,64,64]{3,2,1,0:T(8,128)(2,1)} %param.5) | copy-start | bytes 884740
  2.1 18.7 %copy-start.5 = (s32[3,12,1]{1,2,0:T(1,128)S(1)}, s32[3,12,1]{1,2,0:T(1,128)}, u32[]{:S(2)}) copy-start(s32[3,12,1]{1,2,0:T(1,128)} %param.6) | copy-start | bytes 436
  191.6 14.9 %copy-start.2 = (f32[2,64,128]{2,1,0:T(8,128)S(1)}, f32[2,64,128]{2,1,0:T(8,128)}, u32[]{:S(2)}) copy-start(f32[2,64,128]{2,1,0:T(8,128)} %get-tuple-element.28) | copy-start | bytes 196612
  191.6 14.9 %copy-start.3 = (f32[2,64,128]{2,1,0:T(8,128)S(1)}, f32[2,64,128]{2,1,0:T(8,128)}, u32[]{:S(2)}) copy-start(f32[2,64,128]{2,1,0:T(8,128)} %get-tuple-element.27) | copy-start | bytes 196612
  191.6 14.9 %copy-start.4 = (f32[2,64,128]{2,1,0:T(8,128)S(1)}, f32[2,64,128]{2,1,0:T(8,128)}, u32[]{:S(2)}) copy-start(f32[2,64,128]{2,1,0:T(8,128)} %get-tuple-element.26) | copy-start | bytes 196612

commit v4 on v3

--- a/solution.py
+++ b/solution.py
@@ -21,8 +21,10 @@
     x_ref = refs.pop(0) if ex else None
     base_ref = refs.pop(0)
     g_refs = [refs.pop(0) for _ in applies]
+    if ga:
+        ids_ref, tiles_ref = refs.pop(0), refs.pop(0)
     out_ref = refs.pop(0)
-    gathered_ref = refs.pop(0) if ga else None
+    products_ref = refs.pop(0) if ga else None
     if ex:
         held_x, ex_send, ex_recv = refs.pop(0), refs.pop(0), refs.pop(0)
     if ga:
@@ -88,27 +90,30 @@
                 peer = lax.rem(me + k, n)
                 copy = pltpu.make_async_remote_copy(
                     src_ref=stage.at[kb],
-                    dst_ref=held_g.at[k, kb],
+                    dst_ref=held_g.at[me * blocks + kb],
                     send_sem=ga_send.at[kb, k],
                     recv_sem=ga_recv.at[kb, k],
                     device_id=peer_id(axis, peer),
                     device_id_type=MESH,
                 )
                 copy.start()
-                gather_copies.append((kb, k, copy))
-            gathered_ref[me, kb] = value.astype(gathered_ref.dtype)
-    if ga:
-        axis, n = ga
-        me = lax.axis_index(axis)
-        for kb, k, copy in gather_copies:
+                gather_copies.append(copy)
+            held_g[me * blocks + kb] = value.astype(held_g.dtype)
+    if ga:
+        for copy in gather_copies:
             copy.wait()
-            gathered_ref[lax.rem(me + n - k, n), kb] = held_g[k, kb]
-
-
-def level(cid, x, base, gs, ex=None, ga=None):
+        for t in range(tiles_ref.shape[0]):
+            products_ref[t] = jnp.dot(
+                tiles_ref[t], held_g[ids_ref[t]], preferred_element_type=jnp.float32
+            )
+
+
+def level(cid, x, base, gs, ex=None, ga=None, ids=None, tiles=None):
     piece = base.shape
     vmem = pl.BlockSpec(memory_space=pltpu.VMEM)
+    smem = pl.BlockSpec(memory_space=pltpu.SMEM)
     args = ([x] if ex else []) + [base] + list(gs)
+    specs = [vmem] * len(args)
     out_shape = [jax.ShapeDtypeStruct(piece, jnp.float32)]
     scratch = []
     if ex:
@@ -118,9 +123,11 @@
             pltpu.SemaphoreType.DMA((piece[0], ex[1])),
         ]
     if ga:
-        out_shape.append(jax.ShapeDtypeStruct((ga[1],) + piece, jnp.bfloat16))
+        args += [ids, tiles]
+        specs += [smem, vmem]
+        out_shape.append(jax.ShapeDtypeStruct(tiles.shape[:2] + piece[2:], jnp.float32))
         scratch += [
-            pltpu.VMEM((ga[1],) + piece, jnp.bfloat16),
+            pltpu.VMEM((ga[1] * piece[0],) + piece[1:], jnp.bfloat16),
             pltpu.VMEM(piece, jnp.bfloat16),
             pltpu.SemaphoreType.DMA((piece[0], ga[1])),
             pltpu.SemaphoreType.DMA((piece[0], ga[1])),
@@ -128,7 +135,7 @@
     outs = pl.pallas_call(
         functools.partial(level_kernel, ex, ga, tuple(range(len(gs)))),
         out_shape=out_shape,
-        in_specs=[vmem] * len(args),
+        in_specs=specs,
         out_specs=[vmem] * len(out_shape),
         scratch_shapes=scratch,
         compiler_params=pltpu.CompilerParams(collective_id=cid, has_side_effects=True),
@@ -147,39 +154,41 @@
     g_fwd = split.transpose(0, 2, 3, 1)
     g_bwd = split.transpose(0, 2, 1, 3)
     row_axis, col_axis = ("row", n_row), ("col", n_col)
-
-    current, gathered = level(1, None, right_sides[0], [g_fwd[0]], ga=row_axis)
+    tiles_t = jnp.swapaxes(factor_tiles, 2, 3)
+    places = jnp.arange(n_col * rows_dev, dtype=jnp.int32)
+    columns_here = jnp.arange(group_rows, dtype=jnp.int32)
+
+    def forward_terms(products, section_no):
+        select = (row_ids[section_no][:, None] == places[None, :]).astype(jnp.float32)
+        terms = jnp.einsum("tq,tan->qan", select, products, precision=HIGHEST)
+        return terms.astype(jnp.bfloat16).reshape((n_col, rows_dev) + terms.shape[1:])
+
+    def backward_terms(products, section_no):
+        select = (col_ids[section_no][:, None] == columns_here[None, :]).astype(jnp.float32)
+        sums = jnp.einsum("tj,tbn->jbn", select, products, precision=HIGHEST)
+        return sums.astype(jnp.bfloat16).reshape((n_row, rows_dev) + sums.shape[1:])
+
+    current, products = level(1, None, right_sides[0], [g_fwd[0]], ga=row_axis,
+                              ids=col_ids[0], tiles=factor_tiles[0])
     solved = [current]
     for section_no in range(1, levels + 1):
-        picked = gathered.reshape((group_rows,) + current.shape[1:])[col_ids[section_no - 1]]
-        products = jnp.einsum(
-            "tab,tbn->tan", factor_tiles[section_no - 1], picked, preferred_element_type=jnp.float32
-        )
-        targets = row_ids[section_no - 1]
-        places = jnp.arange(n_col * rows_dev, dtype=jnp.int32)
-        select = (targets[:, None] == places[None, :]).astype(jnp.float32)
-        terms = jnp.einsum("tq,tan->qan", select, products, precision=HIGHEST)
-        terms = terms.astype(jnp.bfloat16).reshape((n_col, rows_dev) + terms.shape[1:])
+        terms = forward_terms(products, section_no - 1)
         if section_no < levels:
-            current, gathered = level(2, terms, right_sides[section_no], [g_fwd[section_no]],
-                                      ex=col_axis, ga=row_axis)
+            current, products = level(2, terms, right_sides[section_no], [g_fwd[section_no]],
+                                      ex=col_axis, ga=row_axis,
+                                      ids=col_ids[section_no], tiles=factor_tiles[section_no])
             solved.append(current)
         else:
-            current, gathered = level(3, terms, right_sides[section_no],
-                                      [g_fwd[section_no], g_bwd[section_no]], ex=col_axis, ga=col_axis)
+            current, products = level(3, terms, right_sides[section_no],
+                                      [g_fwd[section_no], g_bwd[section_no]], ex=col_axis, ga=col_axis,
+                                      ids=row_ids[levels - 1], tiles=tiles_t[levels - 1])
     result = [current]
-    columns_here = jnp.arange(group_rows, dtype=jnp.int32)
     for section_no in range(levels - 1, -1, -1):
-        picked = gathered.reshape((n_col * rows_dev,) + current.shape[1:])[row_ids[section_no]]
-        spread = jnp.einsum(
-            "tab,tan->tbn", factor_tiles[section_no], picked, preferred_element_type=jnp.float32
-        )
-        select = (col_ids[section_no][:, None] == columns_here[None, :]).astype(jnp.float32)
-        column_sums = jnp.einsum("tj,tbn->jbn", select, spread, precision=HIGHEST)
-        column_sums = column_sums.astype(jnp.bfloat16).reshape((n_row, rows_dev) + column_sums.shape[1:])
+        column_sums = backward_terms(products, section_no)
         if section_no > 0:
-            current, gathered = level(4, column_sums, solved[section_no], [g_bwd[section_no]],
-                                      ex=row_axis, ga=col_axis)
+            current, products = level(4, column_sums, solved[section_no], [g_bwd[section_no]],
+                                      ex=row_axis, ga=col_axis,
+                                      ids=row_ids[section_no - 1], tiles=tiles_t[section_no - 1])
         else:
             current, _ = level(5, column_sums, solved[section_no], [g_bwd[section_no]], ex=row_axis)
         result.insert(0, current)

time: 209 us -> 206 us (0.986)
  local copies, waits for them, and re-layouts: 20.3 us -> 12.7 us
  matrix products: 6.41 us -> 11.1 us
    gather x6 -> x0, local copies, waits for them, and re-layouts: 10 us -> none  [the longest x3 5.43 us: solve_all(): gathered.reshape((n_col * rows_dev,) + current.shape[1:])]
    dot_general x12 -> x6, matrix products: 6.41 us -> 11.1 us  [the longest x3 6.31 us: forward_terms(): terms = jnp.einsum('tq,tan->qan', select, products, precision=HIGHEST)]
where the time goes in v4:
time: 206 us
  Pallas kernels  180 us (87%)
  local copies, waits for them, and re-layouts  12.7 us (6%)
  matrix products  11.1 us (5%)
    pallas_call x7, Pallas kernels, level(): pl.pallas_call(functools.partial(level_kernel, ex, ga, tuple(range(len(gs...  180 us
    dot_general x3, matrix products, forward_terms(): terms = jnp.einsum('tq,tan->qan', select, products, precision=HIGHEST)  6.31 us
    convert_element_type x3, local copies, waits for them, and re-layouts, forward_terms(): terms.astype(jnp.bfloat16).reshape((n_col, rows_dev) + terms.shape[1:])  5.01 us
    dot_general x3, matrix products, backward_terms(): sums = jnp.einsum('tj,tbn->jbn', select, products, precision=HIGHEST)  4.74 us

profile of v4, /device:TPU:1, one launch (start us, length us, event | category | flops | bytes accessed | tf_op | source)
XLA Modules:
  0.0 205.5 jit_solution(14135274059915179124)
XLA Ops:
  0.0 1.1 reshape.45
  1.1 0.0 copy-start.1
  1.1 0.1 copy.23
  1.2 0.0 copy-start.11
  1.3 0.0 copy-start
  1.3 0.8 slice_bitcast_fusion.6
  2.1 0.0 copy-start.12
  2.1 0.0 copy-done.1
  2.1 0.7 slice_bitcast_fusion.14
  2.9 0.0 copy-done.11
  2.9 0.6 slice_bitcast_fusion.21
  3.4 0.0 copy-done
  3.4 0.8 slice_bitcast_fusion.3
  4.2 16.5 %shard_map.55 = (f32[2,64,128]{2,1,0:T(8,128)}, f32[12,64,128]{2,1,0:T(8,128)}) custom-call(f32[2,64,128]{2,1,0:T(8,128)} %get-tuple-element.45.refs_0_, f32[2,64,64]{2,1,0:T(8,128)} %get-tuple-element.53.refs_1_, s32[12]{0:T(128)} %get-tuple-element.51.refs_2_, bf16[12,64,64]{2,1,0:T(8,128)(2,1)} %get-tuple-element.34.refs_3_), custom_call_target="tpu_custom_call" | custom-call | tf_op jit(solution)/shard_map/pallas_call | solution.py:135
  20.8 0.0 copy-done.12
  20.8 0.0 copy-start.9
  20.8 0.0 copy-start.10
  20.8 0.0 copy-start.7
  20.8 2.1 %convolution_convert_fusion.2 = bf16[64,64,128]{2,0,1:T(8,128)(2,1)S(1)} fusion(f32[12,64,128]{2,1,0:T(8,128)} %get-tuple-element.17, s32[12]{0:T(128)S(1)} %get-tuple-element.48.refs_3_), kind=kOutput, calls=%fused_computation.2 | convolution fusion | flops 76022528 | bytes 1441840 | tf_op jit(solution)/shard_map/tq,tan->qan/dot_general | solution.py:163
  23.0 1.7 copy.25
  24.6 0.0 copy-done.9
  24.6 32.3 %shard_map.56 = (f32[2,64,128]{2,1,0:T(8,128)}, f32[12,64,128]{2,1,0:T(8,128)}) custom-call(bf16[32,2,64,128]{3,2,1,0:T(8,128)(2,1)} %bitcast.83, f32[2,64,128]{2,1,0:T(8,128)} %get-tuple-element.44.refs_1_, f32[2,64,64]{2,1,0:T(8,128)} %get-tuple-element.54.refs_2_, s32[12]{0:T(128)} %get-tuple-element.52.refs_3_, bf16[12,64,64]{2,1,0:T(8,128)(2,1)} %get-tuple-element.33.refs_4_), custom_call_target="tpu_custom_call" | custom-call | tf_op jit(solution)/shard_map/pallas_call | solution.py:135
  56.9 0.0 copy-done.10
  56.9 2.1 %convolution_convert_fusion.1 = bf16[64,64,128]{2,0,1:T(8,128)(2,1)S(1)} fusion(f32[12,64,128]{2,1,0:T(8,128)} %get-tuple-element.18, s32[12]{0:T(128)S(1)} %get-tuple-element.49.refs_3_), kind=kOutput, calls=%fused_computation.1 | convolution fusion | flops 76022528 | bytes 1441840 | tf_op jit(solution)/shard_map/tq,tan->qan/dot_general | solution.py:163
  59.0 1.7 copy.27
  60.7 26.6 %shard_map.57 = (f32[2,64,128]{2,1,0:T(8,128)}, f32[12,64,128]{2,1,0:T(8,128)}) custom-call(bf16[32,2,64,128]{3,2,1,0:T(8,128)(2,1)} %bitcast.82, f32[2,64,128]{2,1,0:T(8,128)} %get-tuple-element.46.refs_1_, f32[2,64,64]{2,1,0:T(8,128)} %get-tuple-element.55.refs_2_, s32[12]{0:T(128)} %get-tuple-element.50.refs_3_, bf16[12,64,64]{2,1,0:T(8,128)(2,1)} %get-tuple-element.32.refs_4_), custom_call_target="tpu_custom_call" | custom-call | tf_op jit(solution)/shard_map/pallas_call | solution.py:135
  87.3 0.0 copy-done.7
  87.3 2.1 %convolution_convert_fusion = bf16[64,64,128]{2,0,1:T(8,128)(2,1)S(1)} fusion(f32[12,64,128]{2,1,0:T(8,128)} %get-tuple-element.19, s32[12]{0:T(128)S(1)} %get-tuple-element.47.refs_4_), kind=kOutput, calls=%fused_computation | convolution fusion | flops 76022528 | bytes 1441840 | tf_op jit(solution)/shard_map/tq,tan->qan/dot_general | solution.py:163
  89.5 1.7 copy.29
  91.1 0.3 copy.31
  91.4 0.0 copy-start.6
  91.4 0.8 slice_bitcast_fusion
  92.3 34.6 %shard_map.58 = (f32[2,64,128]{2,1,0:T(8,128)}, f32[12,64,128]{2,1,0:T(8,128)}) custom-call(bf16[32,2,64,128]{3,2,1,0:T(8,128)(2,1)} %bitcast.81, f32[2,64,128]{2,1,0:T(8,128)} %get-tuple-element.43.refs_1_, f32[2,64,64]{2,1,0:T(8,128)} %get-tuple-element.56.refs_2_, f32[2,64,64]{2,1,0:T(8,128)} %get-tuple-element.38.refs_3_, s32[12]{0:T(128)} %copy-done.7, ...), custom_call_target="tpu_custom_call" | custom-call | tf_op jit(solution)/shard_map/pallas_call | solution.py:135
  126.8 0.0 copy-start.5
  126.9 0.0 copy-done.6
  126.9 1.6 convolution_convert_fusion.5
  128.4 0.8 copy.33
  129.2 29.5 %shard_map.59 = (f32[2,64,128]{2,1,0:T(8,128)}, f32[12,64,128]{2,1,0:T(8,128)}) custom-call(bf16[8,2,64,128]{3,2,1,0:T(8,128)(2,1)} %bitcast.87, f32[2,64,128]{2,1,0:T(8,128)} %get-tuple-element.21.refs_1_, f32[2,64,64]{2,1,0:T(8,128)} %get-tuple-element.37.refs_2_, s32[12]{0:T(128)} %copy-done.10, bf16[12,64,64]{2,1,0:T(8,128)(2,1)} %get-tuple-element.30.refs_4_), custom_call_target="tpu_custom_call" | custom-call | tf_op jit(solution)/shard_map/pallas_call | solution.py:135
  158.7 0.0 copy-start.8
  158.7 0.0 copy-done.5
  158.7 1.6 convolution_convert_fusion.4
  160.3 0.8 copy.35
  161.1 0.0 copy-start.2
  161.1 0.0 copy-start.3
  161.1 26.3 %shard_map.60 = (f32[2,64,128]{2,1,0:T(8,128)}, f32[12,64,128]{2,1,0:T(8,128)}) custom-call(bf16[8,2,64,128]{3,2,1,0:T(8,128)(2,1)} %bitcast.86, f32[2,64,128]{2,1,0:T(8,128)} %get-tuple-element.23.refs_1_, f32[2,64,64]{2,1,0:T(8,128)} %get-tuple-element.36.refs_2_, s32[12]{0:T(128)} %copy-done.9, bf16[12,64,64]{2,1,0:T(8,128)(2,1)} %get-tuple-element.29.refs_4_), custom_call_target="tpu_custom_call" | custom-call | tf_op jit(solution)/shard_map/pallas_call | solution.py:135
  187.4 0.0 copy-start.4
  187.4 0.0 copy-done.8
  187.4 1.6 convolution_convert_fusion.3
  189.0 0.8 copy.37
  189.8 14.2 %shard_map.61 = f32[2,64,128]{2,1,0:T(8,128)} custom-call(bf16[8,2,64,128]{3,2,1,0:T(8,128)(2,1)} %bitcast.85, f32[2,64,128]{2,1,0:T(8,128)} %get-tuple-element.25.refs_1_, f32[2,64,64]{2,1,0:T(8,128)} %get-tuple-element.35.refs_2_), custom_call_target="tpu_custom_call" | custom-call | tf_op jit(solution)/shard_map/pallas_call | solution.py:135
  203.9 0.0 copy-done.2
  203.9 0.0 copy-done.3
  203.9 0.0 copy-done.4
  204.0 1.6 pad_maximum_fusion
  (2 shorter events, 0.0 us)
Async XLA Ops:
  1.1 1.0 copy-start.1
  1.2 1.6 copy-start.11
  1.3 2.2 %copy-start = (bf16[3,12,64,64]{3,2,1,0:T(8,128)(2,1)S(1)}, bf16[3,12,64,64]{3,2,1,0:T(8,128)(2,1)}, u32[]{:S(2)}) copy-start(bf16[3,12,64,64]{3,2,1,0:T(8,128)(2,1)} %param.5) | copy-start | bytes 884740
  2.1 18.7 %copy-start.12 = (s32[3,12,1]{1,2,0:T(1,128)S(1)}, s32[3,12,1]{1,2,0:T(1,128)}, u32[]{:S(2)}) copy-start(s32[3,12,1]{1,2,0:T(1,128)} %param.6) | copy-start | bytes 436
  20.8 3.8 %copy-start.9 = (s32[12]{0:T(128)}, s32[12]{0:T(128)S(1)}, u32[]{:S(2)}) copy-start(s32[12]{0:T(128)S(1)} %get-tuple-element.48.refs_3_) | copy-start | bytes 148
  20.8 36.1 %copy-start.10 = (s32[12]{0:T(128)}, s32[12]{0:T(128)S(1)}, u32[]{:S(2)}) copy-start(s32[12]{0:T(128)S(1)} %get-tuple-element.49.refs_3_) | copy-start | bytes 148
  20.8 66.5 %copy-start.7 = (s32[12]{0:T(128)}, s32[12]{0:T(128)S(1)}, u32[]{:S(2)}) copy-start(s32[12]{0:T(128)S(1)} %get-tuple-element.47.refs_4_) | copy-start | bytes 148
  91.4 35.4 %copy-start.6 = (s32[12]{0:T(128)S(1)}, s32[12]{0:T(128)}, u32[]{:S(2)}) copy-start(s32[12]{0:T(128)} %get-tuple-element.50.refs_3_) | copy-start | bytes 148
  126.8 31.9 %copy-start.5 = (s32[12]{0:T(128)S(1)}, s32[12]{0:T(128)}, u32[]{:S(2)}) copy-start(s32[12]{0:T(128)} %get-tuple-element.52.refs_3_) | copy-start | bytes 148
  158.7 28.7 %copy-start.8 = (s32[12]{0:T(128)S(1)}, s32[12]{0:T(128)}, u32[]{:S(2)}) copy-start(s32[12]{0:T(128)} %get-tuple-element.51.refs_2_) | copy-start | bytes 148
  161.1 42.9 %copy-start.2 = (f32[2,64,128]{2,1,0:T(8,128)S(1)}, f32[2,64,128]{2,1,0:T(8,128)}, u32[]{:S(2)}) copy-start(f32[2,64,128]{2,1,0:T(8,128)} %get-tuple-element.28) | copy-start | bytes 196612
  161.1 42.9 %copy-start.3 = (f32[2,64,128]{2,1,0:T(8,128)S(1)}, f32[2,64,128]{2,1,0:T(8,128)}, u32[]{:S(2)}) copy-start(f32[2,64,128]{2,1,0:T(8,128)} %get-tuple-element.27) | copy-start | bytes 196612
  187.4 16.6 %copy-start.4 = (f32[2,64,128]{2,1,0:T(8,128)S(1)}, f32[2,64,128]{2,1,0:T(8,128)}, u32[]{:S(2)}) copy-start(f32[2,64,128]{2,1,0:T(8,128)} %get-tuple-element.26) | copy-start | bytes 196612

commit v5 on v4

--- a/solution.py
+++ b/solution.py
@@ -22,13 +22,13 @@
     base_ref = refs.pop(0)
     g_refs = [refs.pop(0) for _ in applies]
     if ga:
-        ids_ref, tiles_ref = refs.pop(0), refs.pop(0)
+        ids_ref, tiles_ref, key_ref, first_ref, has_ref = [refs.pop(0) for _ in range(5)]
     out_ref = refs.pop(0)
-    products_ref = refs.pop(0) if ga else None
+    terms_ref = refs.pop(0) if ga else None
     if ex:
         held_x, ex_send, ex_recv = refs.pop(0), refs.pop(0), refs.pop(0)
     if ga:
-        held_g, stage, ga_send, ga_recv = refs.pop(0), refs.pop(0), refs.pop(0), refs.pop(0)
+        held_g, stage, ga_send, ga_recv, prod, group = [refs.pop(0) for _ in range(6)]
     blocks = base_ref.shape[0]
 
     groups = [g for g in (ex, ga) if g]
@@ -102,13 +102,32 @@
     if ga:
         for copy in gather_copies:
             copy.wait()
-        for t in range(tiles_ref.shape[0]):
-            products_ref[t] = jnp.dot(
-                tiles_ref[t], held_g[ids_ref[t]], preferred_element_type=jnp.float32
-            )
-
-
-def level(cid, x, base, gs, ex=None, ga=None, ids=None, tiles=None):
+        tiles = tiles_ref.shape[0]
+
+        def product(t, carry):
+            prod[t] = jnp.dot(tiles_ref[t], held_g[ids_ref[t]], preferred_element_type=jnp.float32)
+            return carry
+
+        lax.fori_loop(0, tiles, product, 0)
+
+        def grouping(t, carry):
+            key = key_ref[t]
+            acc = jnp.zeros(prod.shape[1:], jnp.float32)
+            for other in range(tiles):
+                acc = acc + jnp.where(key_ref[other] == key, prod[other], 0.0)
+            group[t] = acc
+            return carry
+
+        lax.fori_loop(0, tiles, grouping, 0)
+
+        def place(q, carry):
+            terms_ref[q] = (group[first_ref[q]] * has_ref[q]).astype(terms_ref.dtype)
+            return carry
+
+        lax.fori_loop(0, terms_ref.shape[0], place, 0)
+
+
+def level(cid, x, base, gs, ex=None, ga=None, ids=None, tiles=None, keys=None):
     piece = base.shape
     vmem = pl.BlockSpec(memory_space=pltpu.VMEM)
     smem = pl.BlockSpec(memory_space=pltpu.SMEM)
@@ -123,14 +142,17 @@
             pltpu.SemaphoreType.DMA((piece[0], ex[1])),
         ]
     if ga:
-        args += [ids, tiles]
-        specs += [smem, vmem]
-        out_shape.append(jax.ShapeDtypeStruct(tiles.shape[:2] + piece[2:], jnp.float32))
+        key, first, has = keys
+        args += [ids, tiles, key, first, has]
+        specs += [smem, vmem, smem, smem, smem]
+        out_shape.append(jax.ShapeDtypeStruct(first.shape + piece[1:], jnp.bfloat16))
         scratch += [
             pltpu.VMEM((ga[1] * piece[0],) + piece[1:], jnp.bfloat16),
             pltpu.VMEM(piece, jnp.bfloat16),
             pltpu.SemaphoreType.DMA((piece[0], ga[1])),
             pltpu.SemaphoreType.DMA((piece[0], ga[1])),
+            pltpu.VMEM(tiles.shape[:2] + piece[2:], jnp.float32),
+            pltpu.VMEM(tiles.shape[:2] + piece[2:], jnp.float32),
         ]
     outs = pl.pallas_call(
         functools.partial(level_kernel, ex, ga, tuple(range(len(gs)))),
@@ -155,42 +177,44 @@
     g_bwd = split.transpose(0, 2, 1, 3)
     row_axis, col_axis = ("row", n_row), ("col", n_col)
     tiles_t = jnp.swapaxes(factor_tiles, 2, 3)
-    places = jnp.arange(n_col * rows_dev, dtype=jnp.int32)
-    columns_here = jnp.arange(group_rows, dtype=jnp.int32)
-
-    def forward_terms(products, section_no):
-        select = (row_ids[section_no][:, None] == places[None, :]).astype(jnp.float32)
-        terms = jnp.einsum("tq,tan->qan", select, products, precision=HIGHEST)
-        return terms.astype(jnp.bfloat16).reshape((n_col, rows_dev) + terms.shape[1:])
-
-    def backward_terms(products, section_no):
-        select = (col_ids[section_no][:, None] == columns_here[None, :]).astype(jnp.float32)
-        sums = jnp.einsum("tj,tbn->jbn", select, products, precision=HIGHEST)
-        return sums.astype(jnp.bfloat16).reshape((n_row, rows_dev) + sums.shape[1:])
-
-    current, products = level(1, None, right_sides[0], [g_fwd[0]], ga=row_axis,
-                              ids=col_ids[0], tiles=factor_tiles[0])
+
+    def grouping(keys, size):
+        hits = keys[:, :, None] == jnp.arange(size, dtype=jnp.int32)[None, None, :]
+        return keys, jnp.argmax(hits, axis=1).astype(jnp.int32), jnp.any(hits, axis=1).astype(jnp.float32)
+
+    fwd_keys = grouping(row_ids, n_col * rows_dev)
+    bwd_keys = grouping(col_ids, group_rows)
+
+    def keys_of(which, section_no):
+        return tuple(k[section_no] for k in which)
+
+    def as_pieces(terms, n):
+        return terms.reshape((n, rows_dev) + terms.shape[1:])
+
+    current, terms = level(1, None, right_sides[0], [g_fwd[0]], ga=row_axis,
+                           ids=col_ids[0], tiles=factor_tiles[0], keys=keys_of(fwd_keys, 0))
     solved = [current]
     for section_no in range(1, levels + 1):
-        terms = forward_terms(products, section_no - 1)
+        terms = as_pieces(terms, n_col)
         if section_no < levels:
-            current, products = level(2, terms, right_sides[section_no], [g_fwd[section_no]],
-                                      ex=col_axis, ga=row_axis,
-                                      ids=col_ids[section_no], tiles=factor_tiles[section_no])
+            current, terms = level(2, terms, right_sides[section_no], [g_fwd[section_no]],
+                                   ex=col_axis, ga=row_axis, ids=col_ids[section_no],
+                                   tiles=factor_tiles[section_no], keys=keys_of(fwd_keys, section_no))
             solved.append(current)
         else:
-            current, products = level(3, terms, right_sides[section_no],
-                                      [g_fwd[section_no], g_bwd[section_no]], ex=col_axis, ga=col_axis,
-                                      ids=row_ids[levels - 1], tiles=tiles_t[levels - 1])
+            current, terms = level(3, terms, right_sides[section_no],
+                                   [g_fwd[section_no], g_bwd[section_no]], ex=col_axis, ga=col_axis,
+                                   ids=row_ids[levels - 1], tiles=tiles_t[levels - 1],
+                                   keys=keys_of(bwd_keys, levels - 1))
     result = [current]
     for section_no in range(levels - 1, -1, -1):
-        column_sums = backward_terms(products, section_no)
+        terms = as_pieces(terms, n_row)
         if section_no > 0:
-            current, products = level(4, column_sums, solved[section_no], [g_bwd[section_no]],
-                                      ex=row_axis, ga=col_axis,
-                                      ids=row_ids[section_no - 1], tiles=tiles_t[section_no - 1])
+            current, terms = level(4, terms, solved[section_no], [g_bwd[section_no]],
+                                   ex=row_axis, ga=col_axis, ids=row_ids[section_no - 1],
+                                   tiles=tiles_t[section_no - 1], keys=keys_of(bwd_keys, section_no - 1))
         else:
-            current, _ = level(5, column_sums, solved[section_no], [g_bwd[section_no]], ex=row_axis)
+            current, _ = level(5, terms, solved[section_no], [g_bwd[section_no]], ex=row_axis)
         result.insert(0, current)
     return jnp.stack(result)
 

time: 206 us -> 204 us (level)
  Pallas kernels: 180 us -> 192 us
  matrix products: 11.1 us -> 0 us
  local copies, waits for them, and re-layouts: 12.7 us -> 8.38 us
    pallas_call x7, Pallas kernels: 180 us -> 192 us  [level(): pl.pallas_call(functools.partial(level_kernel, ex, ga, tuple(range(len(gs...]
    dot_general x6 -> x0, matrix products: 11.1 us -> none  [the longest x3 6.31 us: forward_terms(): terms = jnp.einsum('tq,tan->qan', select, products, precision=HIGHEST)]
    convert_element_type x6 -> x0, local copies, waits for them, and re-layouts: 7.33 us -> none  [the longest x3 5.01 us: forward_terms(): terms.astype(jnp.bfloat16).reshape((n_col, rows_dev) + terms.shape[1:])]
    squeeze x0 -> x5, local copies, waits for them, and re-layouts: none -> 2.95 us  [keys_of(): return tuple((k[section_no] for k in which))]
where the time goes in v5:
time: 204 us; the launch traced here: 203 us
  Pallas kernels  192 us (94%)
  local copies, waits for them, and re-layouts  8.38 us (4%)
  other arithmetic  2.98 us (1%)
    pallas_call x7, Pallas kernels, level(): pl.pallas_call(functools.partial(level_kernel, ex, ga, tuple(range(len(gs...  192 us

profile of v5, /device:TPU:1, one launch (start us, length us, event | category | flops | bytes accessed | tf_op | source)
XLA Modules:
  0.0 203.1 jit_solution(5719217219649556987)
XLA Ops:
  0.0 1.1 reshape.33
  1.1 0.1 copy.14
  1.3 0.0 copy-start.6
  1.3 0.0 copy-start.1
  1.3 0.0 copy-start
  1.3 0.8 slice_bitcast_fusion.6
  2.1 0.0 copy-start.5
  2.1 0.0 copy-done.6
  2.1 0.7 copy-done.5
  2.8 0.6 slice_bitcast_fusion.26
  3.4 0.0 copy-done.1
  3.4 0.7 slice_bitcast_fusion.14
  4.1 0.6 iota_reduce_fusion.1
  4.7 0.6 slice_bitcast_fusion.25
  5.3 0.1 fusion.1
  5.4 0.6 slice_bitcast_fusion.24
  6.0 0.0 copy-done
  6.0 0.8 slice_bitcast_fusion.3
  6.9 19.0 %shard_map.55 = (f32[2,64,128]{2,1,0:T(8,128)}, bf16[64,64,128]{2,1,0:T(8,128)(2,1)}) custom-call(f32[2,64,128]{2,1,0:T(8,128)} %get-tuple-element.49.refs_0_, f32[2,64,64]{2,1,0:T(8,128)} %get-tuple-element.72.refs_1_, s32[12]{0:T(128)} %get-tuple-element.69.refs_2_.refs_5_, bf16[12,64,64]{2,1,0:T(8,128)(2,1)} %get-tuple-element.38.refs_3_, ...), custom_call_target="tpu_custom_call" | custom-call | tf_op jit(solution)/shard_map/pallas_call | solution.py:157
  25.9 34.9 %shard_map.56 = (f32[2,64,128]{2,1,0:T(8,128)}, bf16[64,64,128]{2,1,0:T(8,128)(2,1)}) custom-call(bf16[32,2,64,128]{3,2,1,0:T(8,128)(2,1)} %bitcast.96, f32[2,64,128]{2,1,0:T(8,128)} %get-tuple-element.48.refs_1_, f32[2,64,64]{2,1,0:T(8,128)} %get-tuple-element.73.refs_2_, s32[12]{0:T(128)} %get-tuple-element.70.refs_3_.refs_5_, ...), custom_call_target="tpu_custom_call" | custom-call | tf_op jit(solution)/shard_map/pallas_call | solution.py:157
  60.8 29.2 %shard_map.57 = (f32[2,64,128]{2,1,0:T(8,128)}, bf16[64,64,128]{2,1,0:T(8,128)(2,1)}) custom-call(bf16[32,2,64,128]{3,2,1,0:T(8,128)(2,1)} %bitcast.95, f32[2,64,128]{2,1,0:T(8,128)} %get-tuple-element.50.refs_1_, f32[2,64,64]{2,1,0:T(8,128)} %get-tuple-element.74.refs_2_, s32[12]{0:T(128)} %get-tuple-element.71.refs_3_.refs_6_, ...), custom_call_target="tpu_custom_call" | custom-call | tf_op jit(solution)/shard_map/pallas_call | solution.py:157
  90.0 0.6 iota_reduce_fusion
  90.6 0.6 slice_bitcast_fusion.19
  91.1 0.1 fusion
  91.2 0.6 slice_bitcast_fusion.18
  91.8 0.3 copy.16
  92.1 0.8 slice_bitcast_fusion
  92.9 36.7 %shard_map.58 = (f32[2,64,128]{2,1,0:T(8,128)}, bf16[16,64,128]{2,1,0:T(8,128)(2,1)}) custom-call(bf16[32,2,64,128]{3,2,1,0:T(8,128)(2,1)} %bitcast.94, f32[2,64,128]{2,1,0:T(8,128)} %get-tuple-element.47.refs_1_, f32[2,64,64]{2,1,0:T(8,128)} %get-tuple-element.75.refs_2_, f32[2,64,64]{2,1,0:T(8,128)} %get-tuple-element.42.refs_3_, ...), custom_call_target="tpu_custom_call" | custom-call | tf_op jit(solution)/shard_map/pallas_call | solution.py:157
  129.7 30.3 %shard_map.59 = (f32[2,64,128]{2,1,0:T(8,128)}, bf16[16,64,128]{2,1,0:T(8,128)(2,1)}) custom-call(bf16[8,2,64,128]{3,2,1,0:T(8,128)(2,1)} %bitcast.101, f32[2,64,128]{2,1,0:T(8,128)} %get-tuple-element.25.refs_1_, f32[2,64,64]{2,1,0:T(8,128)} %get-tuple-element.41.refs_2_, s32[12]{0:T(128)} %get-tuple-element.65.refs_5_.refs_3_, ...), custom_call_target="tpu_custom_call" | custom-call | tf_op jit(solution)/shard_map/pallas_call | solution.py:157
  160.0 28.3 %shard_map.60 = (f32[2,64,128]{2,1,0:T(8,128)}, bf16[16,64,128]{2,1,0:T(8,128)(2,1)}) custom-call(bf16[8,2,64,128]{3,2,1,0:T(8,128)(2,1)} %bitcast.100, f32[2,64,128]{2,1,0:T(8,128)} %get-tuple-element.27.refs_1_, f32[2,64,64]{2,1,0:T(8,128)} %get-tuple-element.40.refs_2_, s32[12]{0:T(128)} %get-tuple-element.64.refs_4_.refs_3_, ...), custom_call_target="tpu_custom_call" | custom-call | tf_op jit(solution)/shard_map/pallas_call | solution.py:157
  188.3 0.0 copy-start.2
  188.3 0.0 copy-start.3
  188.3 0.0 copy-start.4
  188.3 13.2 %shard_map.61 = f32[2,64,128]{2,1,0:T(8,128)} custom-call(bf16[8,2,64,128]{3,2,1,0:T(8,128)(2,1)} %bitcast.99, f32[2,64,128]{2,1,0:T(8,128)} %get-tuple-element.29.refs_1_, f32[2,64,64]{2,1,0:T(8,128)} %get-tuple-element.39.refs_2_), custom_call_target="tpu_custom_call" | custom-call | tf_op jit(solution)/shard_map/pallas_call | solution.py:157
  201.5 0.0 copy-done.2
  201.6 0.0 copy-done.3
  201.6 0.0 copy-done.4
  201.6 1.6 pad_maximum_fusion
  (5 shorter events, 0.0 us)
Async XLA Ops:
  1.3 0.8 copy-start.6
  1.3 2.1 %copy-start.1 = (f32[4,2,64,128]{3,2,1,0:T(8,128)S(1)}, f32[4,2,64,128]{3,2,1,0:T(8,128)}, u32[]{:S(2)}) copy-start(f32[4,2,64,128]{3,2,1,0:T(8,128)} %param.8) | copy-start | bytes 786436
  1.3 4.7 %copy-start = (bf16[3,12,64,64]{3,2,1,0:T(8,128)(2,1)S(1)}, bf16[3,12,64,64]{3,2,1,0:T(8,128)(2,1)}, u32[]{:S(2)}) copy-start(bf16[3,12,64,64]{3,2,1,0:T(8,128)(2,1)} %param.5) | copy-start | bytes 884740
  2.1 0.7 copy-start.5
  188.3 13.3 %copy-start.2 = (f32[2,64,128]{2,1,0:T(8,128)S(1)}, f32[2,64,128]{2,1,0:T(8,128)}, u32[]{:S(2)}) copy-start(f32[2,64,128]{2,1,0:T(8,128)} %get-tuple-element.32) | copy-start | bytes 196612
  188.3 13.3 %copy-start.3 = (f32[2,64,128]{2,1,0:T(8,128)S(1)}, f32[2,64,128]{2,1,0:T(8,128)}, u32[]{:S(2)}) copy-start(f32[2,64,128]{2,1,0:T(8,128)} %get-tuple-element.31) | copy-start | bytes 196612
  188.3 13.3 %copy-start.4 = (f32[2,64,128]{2,1,0:T(8,128)S(1)}, f32[2,64,128]{2,1,0:T(8,128)}, u32[]{:S(2)}) copy-start(f32[2,64,128]{2,1,0:T(8,128)} %get-tuple-element.30) | copy-start | bytes 196612

commit v6 on v3

v6 whole, which is shorter than its diff:
```python
import functools

import jax
import jax.numpy as jnp
from jax import lax
from jax.experimental import pallas as pl
from jax.experimental.pallas import tpu as pltpu
from jax.sharding import PartitionSpec as P

MESH = pl.DeviceIdType.MESH
AXES = ("row", "col")
HIGHEST = lax.Precision.HIGHEST


def peer_id(axis, peer):
    return tuple(peer if name == axis else lax.axis_index(name) for name in AXES)


def phase(cfg, base, gs, out, x, ids, tiles, keys, bufs):
    ex, ga = cfg
    blocks = base.shape[0]

    def exchange_copies(kb):
        axis, n = ex
        held_x, ex_send, ex_recv = bufs["ex"]
        me = lax.axis_index(axis)
        copies = []
        for k in range(1, n):
            peer = lax.rem(me + k, n)
            copy = pltpu.make_async_remote_copy(
                src_ref=x.at[peer, kb],
                dst_ref=held_x.at[k, kb],
                send_sem=ex_send.at[kb, k],
                recv_sem=ex_recv.at[kb, k],
                device_id=peer_id(axis, peer),
                device_id_type=MESH,
            )
            copy.start()
            copies.append(copy)
        return copies

    gather_copies = []
    pending = exchange_copies(0) if ex else None
    for kb in range(blocks):
        value = base[kb]
        if ex:
            axis, n = ex
            held_x = bufs["ex"][0]
            me = lax.axis_index(axis)
            copies = pending
            if kb + 1 < blocks:
                for copy in copies:
                    copy.wait_send()
                pending = exchange_copies(kb + 1)
            total = x[me, kb].astype(jnp.float32)
            for k in range(1, n):
                copies[k - 1].wait_recv()
                total = total + held_x[k, kb].astype(jnp.float32)
            if kb + 1 == blocks:
                for copy in copies:
                    copy.wait_send()
            value = value - total
        for g in gs:
            value = jnp.dot(g[kb], value, precision=HIGHEST, preferred_element_type=jnp.float32)
        out[kb] = value
        if ga:
            axis, n = ga
            held_g, stage, ga_send, ga_recv, _ = bufs["ga"]
            me = lax.axis_index(axis)
            stage[kb] = value.astype(stage.dtype)
            for k in range(1, n):
                peer = lax.rem(me + k, n)
                copy = pltpu.make_async_remote_copy(
                    src_ref=stage.at[kb],
                    dst_ref=held_g.at[me * blocks + kb],
                    send_sem=ga_send.at[kb, k],
                    recv_sem=ga_recv.at[kb, k],
                    device_id=peer_id(axis, peer),
                    device_id_type=MESH,
                )
                copy.start()
                gather_copies.append(copy)
            held_g[me * blocks + kb] = value.astype(held_g.dtype)
    if not ga:
        return
    held_g, _, _, _, terms = bufs["ga"]
    prod, group = bufs["work"]
    for copy in gather_copies:
        copy.wait()
    n_tiles = prod.shape[0]

    def product(t, carry):
        prod[t] = jnp.dot(tiles[t], held_g[ids[t]], preferred_element_type=jnp.float32)
        return carry

    lax.fori_loop(0, n_tiles, product, 0)
    key, first, has = keys

    def grouping(t, carry):
        mine = key[t]
        acc = jnp.zeros(prod.shape[1:], jnp.float32)
        for other in range(n_tiles):
            acc = acc + jnp.where(key[other] == mine, prod[other], 0.0)
        group[t] = acc
        return carry

    lax.fori_loop(0, n_tiles, grouping, 0)

    def place(q, carry):
        terms[q // blocks, q % blocks] = (group[first[q]] * has[q]).astype(terms.dtype)
        return carry

    lax.fori_loop(0, terms.shape[0] * blocks, place, 0)


def solve_kernel(plan, *refs):
    refs = list(refs)
    (rhs, g_fwd, g_bwd, tiles, tiles_t, row_ids, col_ids,
     fwd_first, fwd_has, bwd_first, bwd_has, out, prod, group) = [refs.pop(0) for _ in range(14)]
    bufs = []
    for ex, ga in plan:
        entry = {"work": (prod, group)}
        if ex:
            entry["ex"] = tuple(refs.pop(0) for _ in range(3))
        if ga:
            entry["ga"] = tuple(refs.pop(0) for _ in range(5))
        bufs.append(entry)

    peers = {}
    for ex, ga in plan:
        for group_axis in (ex, ga):
            if group_axis:
                peers[group_axis[0]] = group_axis[1]
    barrier = pltpu.get_barrier_semaphore()
    for axis, n in peers.items():
        me = lax.axis_index(axis)
        for k in range(1, n):
            pl.semaphore_signal(
                barrier, inc=1, device_id=peer_id(axis, lax.rem(me + k, n)), device_id_type=MESH
            )
    pl.semaphore_wait(barrier, sum(n - 1 for n in peers.values()))

    levels = tiles.shape[0]

    def fwd_keys(s):
        return row_ids.at[s], fwd_first.at[s], fwd_has.at[s]

    def bwd_keys(s):
        return col_ids.at[s], bwd_first.at[s], bwd_has.at[s]

    previous = None
    for p, cfg in enumerate(plan):
        x = previous
        if p < levels:
            phase(cfg, rhs.at[p], [g_fwd.at[p]], out.at[p], x, col_ids.at[p], tiles.at[p],
                  fwd_keys(p), bufs[p])
        elif p == levels:
            phase(cfg, rhs.at[p], [g_fwd.at[p], g_bwd.at[p]], out.at[p], x, row_ids.at[p - 1],
                  tiles_t.at[p - 1], bwd_keys(p - 1), bufs[p])
        else:
            s = 2 * levels - p
            if s > 0:
                phase(cfg, out.at[s], [g_bwd.at[s]], out.at[s], x, row_ids.at[s - 1], tiles_t.at[s - 1],
                      bwd_keys(s - 1), bufs[p])
            else:
                phase(cfg, out.at[s], [g_bwd.at[s]], out.at[s], x, None, None, None, bufs[p])
        if cfg[1]:
            previous = bufs[p]["ga"][4]


def solve_all(n_row, n_col, factor_tiles, tile_row, tile_col, right_sides, diag_inverse):
    levels = factor_tiles.shape[0]
    rows_dev = right_sides.shape[1]
    block = right_sides.shape[2]
    group_rows = rows_dev * n_row
    row_ids = tile_row[:, :, 0]
    col_ids = tile_col[:, :, 0]
    split = diag_inverse.reshape(levels + 1, block, rows_dev, block)
    g_fwd = split.transpose(0, 2, 3, 1)
    g_bwd = split.transpose(0, 2, 1, 3)
    tiles_t = jnp.swapaxes(factor_tiles, 2, 3)
    row_axis, col_axis = ("row", n_row), ("col", n_col)

    def grouping(keys, size):
        hits = keys[:, :, None] == jnp.arange(size, dtype=jnp.int32)[None, None, :]
        return jnp.argmax(hits, axis=1).astype(jnp.int32), jnp.any(hits, axis=1).astype(jnp.float32)

    fwd_first, fwd_has = grouping(row_ids, n_col * rows_dev)
    bwd_first, bwd_has = grouping(col_ids, group_rows)

    plan = [(None, row_axis)]
    plan += [(col_axis, row_axis)] * (levels - 1)
    plan += [(col_axis, col_axis)]
    plan += [(row_axis, col_axis)] * (levels - 1)
    plan += [(row_axis, None)]

    piece = right_sides.shape[1:]
    n_tiles = factor_tiles.shape[1]
    vmem = pl.BlockSpec(memory_space=pltpu.VMEM)
    smem = pl.BlockSpec(memory_space=pltpu.SMEM)
    scratch = [
        pltpu.VMEM((n_tiles,) + piece[1:], jnp.float32),
        pltpu.VMEM((n_tiles,) + piece[1:], jnp.float32),
    ]
    for ex, ga in plan:
        if ex:
            scratch += [
                pltpu.VMEM((ex[1],) + piece, jnp.bfloat16),
                pltpu.SemaphoreType.DMA((rows_dev, ex[1])),
                pltpu.SemaphoreType.DMA((rows_dev, ex[1])),
            ]
        if ga:
            targets = n_col if ga[0] == "row" else n_row
            scratch += [
                pltpu.VMEM((ga[1] * rows_dev,) + piece[1:], jnp.bfloat16),
                pltpu.VMEM(piece, jnp.bfloat16),
                pltpu.SemaphoreType.DMA((rows_dev, ga[1])),
                pltpu.SemaphoreType.DMA((rows_dev, ga[1])),
                pltpu.VMEM((targets,) + piece, jnp.bfloat16),
            ]
    args = [right_sides, g_fwd, g_bwd, factor_tiles, tiles_t, row_ids, col_ids,
            fwd_first, fwd_has, bwd_first, bwd_has]
    specs = [vmem] * 5 + [smem] * 6
    return pl.pallas_call(
        functools.partial(solve_kernel, plan),
        out_shape=jax.ShapeDtypeStruct(right_sides.shape, jnp.float32),
        in_specs=specs,
        out_specs=vmem,
        scratch_shapes=scratch,
        compiler_params=pltpu.CompilerParams(collective_id=1, has_side_effects=True),
    )(*args)


def solution(mesh):
    n_row, n_col = mesh.shape["row"], mesh.shape["col"]
    return jax.shard_map(
        functools.partial(solve_all, n_row, n_col),
        mesh=mesh,
        in_specs=(
            P(None, "row", None, "col"),
            P(None, "row", "col"),
            P(None, "row", "col"),
            P(None, ("col", "row"), None, None),
            P(None, None, ("col", "row")),
        ),
        out_specs=P(None, ("col", "row"), None, None),
        check_vma=False,
    )
```

time: 209 us -> 169 us (0.81)
  Pallas kernels: 179 us -> 160 us
  local copies, waits for them, and re-layouts: 20.3 us -> 6.06 us
  matrix products: 6.41 us -> 0 us
    pallas_call x7 -> x1, Pallas kernels: 179 us -> 160 us  [solve_all(): pl.pallas_call(functools.partial(solve_kernel, plan), out_shape=jax.Shape...]
    gather x6 -> x0, local copies, waits for them, and re-layouts: 10 us -> none  [the longest x3 5.43 us: solve_all(): gathered.reshape((n_col * rows_dev,) + current.shape[1:])]
    convert_element_type x6 -> x0, local copies, waits for them, and re-layouts: 7.51 us -> none  [the longest x3 5.01 us: solve_all(): terms.astype(jnp.bfloat16).reshape((n_col, rows_dev) + terms.shape[1:])]
    dot_general x12 -> x0, matrix products: 6.41 us -> none  [the longest x3 3.32 us: solve_all(): terms = jnp.einsum('tq,tan->qan', select, products, precision=HIGHEST)]
    unnamed x14 -> x9, local copies, waits for them, and re-layouts: 0.04 us -> 3.42 us
where the time goes in v6:
time: 169 us
  Pallas kernels  160 us (95%)
  local copies, waits for them, and re-layouts  6.06 us (4%)
  other arithmetic  2.7 us (2%)
    pallas_call x1, Pallas kernels, solve_all(): pl.pallas_call(functools.partial(solve_kernel, plan), out_shape=jax.Shape...  160 us
    unnamed x9, local copies, waits for them, and re-layouts  3.42 us

profile of v6, /device:TPU:1, one launch (start us, length us, event | category | flops | bytes accessed | tf_op | source)
XLA Modules:
  0.0 168.9 jit_solution(12255040080025545251)
XLA Ops:
  0.0 0.7 copy_bitcast_fusion.1
  0.7 0.0 copy-start.1
  0.7 0.0 copy-start.2
  0.7 0.1 fusion
  0.8 0.1 fusion.1
  0.9 0.6 convert_element_type.6.refs_8_
  1.5 0.6 convert_element_type.7.refs_10_
  2.0 0.0 copy-done.1
  2.0 0.7 iota_reduce_fusion
  2.7 0.0 copy-done.2
  2.7 0.7 iota_reduce_fusion.1
  3.4 1.1 reshape.3
  4.5 0.0 copy-start
  4.5 0.7 copy.19
  5.2 0.8 copy.11
  6.1 0.0 copy-done
  6.1 1.0 copy.13
  7.1 160.1 %shard_map.55 = f32[4,2,64,128]{3,2,1,0:T(8,128)} custom-call(f32[4,2,64,128]{3,2,1,0:T(8,128)} %refs_0_.1, f32[4,2,64,64]{3,2,1,0:T(8,128)} %bitcast.11, f32[4,2,64,64]{3,2,1,0:T(8,128)} %bitcast.10, bf16[3,12,64,64]{3,2,1,0:T(8,128)(2,1)} %refs_3_.1, bf16[3,12,64,64]{3,2,1,0:T(8,128)(2,1)} %bitcast.9, s32[3,12]{1,0:T(4,128)} %copy-done.2, ...), custom_call_target="tpu_custom_call" | custom-call | tf_op jit(solution)/shard_map/pallas_call | solution.py:224
  167.2 1.7 copy.21
Async XLA Ops:
  0.7 1.3 copy-start.1
  0.7 2.0 %copy-start.2 = (s32[3,12]{1,0:T(4,128)}, s32[3,12]{1,0:T(4,128)S(1)}, u32[]{:S(2)}) copy-start(s32[3,12]{1,0:T(4,128)S(1)} %get-tuple-element.10.refs_5_) | copy-start | bytes 436
  4.5 1.6 copy-start

commit v7 on v6

--- a/solution.py
+++ b/solution.py
@@ -16,7 +16,7 @@
     return tuple(peer if name == axis else lax.axis_index(name) for name in AXES)
 
 
-def phase(cfg, base, gs, out, x, ids, tiles, keys, bufs):
+def phase(cfg, base, gs, out, x, ids, tiles, keys, bufs, tiles_transposed=False, meanwhile=None):
     ex, ga = cfg
     blocks = base.shape[0]
 
@@ -60,8 +60,12 @@
                 for copy in copies:
                     copy.wait_send()
             value = value - total
-        for g in gs:
-            value = jnp.dot(g[kb], value, precision=HIGHEST, preferred_element_type=jnp.float32)
+        width = value.shape[0]
+        for diag, transposed in gs:
+            d = diag[:, pl.ds(kb * width, width)]
+            contract = 0 if transposed else 1
+            value = lax.dot_general(d, value, (((contract,), (0,)), ((), ())),
+                                    precision=HIGHEST, preferred_element_type=jnp.float32)
         out[kb] = value
         if ga:
             axis, n = ga
@@ -85,38 +89,60 @@
         return
     held_g, _, _, _, terms = bufs["ga"]
     prod, group = bufs["work"]
+    if meanwhile is not None:
+        meanwhile()
     for copy in gather_copies:
         copy.wait()
     n_tiles = prod.shape[0]
 
     def product(t, carry):
-        prod[t] = jnp.dot(tiles[t], held_g[ids[t]], preferred_element_type=jnp.float32)
+        contract = 0 if tiles_transposed else 1
+        prod[t] = lax.dot_general(tiles[t], held_g[ids[t, 0]], (((contract,), (0,)), ((), ())),
+                                  preferred_element_type=jnp.float32)
         return carry
 
     lax.fori_loop(0, n_tiles, product, 0)
     key, first, has = keys
 
     def grouping(t, carry):
-        mine = key[t]
+        mine = key[t, 0]
         acc = jnp.zeros(prod.shape[1:], jnp.float32)
         for other in range(n_tiles):
-            acc = acc + jnp.where(key[other] == mine, prod[other], 0.0)
+            acc = acc + jnp.where(key[other, 0] == mine, prod[other], 0.0)
         group[t] = acc
         return carry
 
     lax.fori_loop(0, n_tiles, grouping, 0)
 
     def place(q, carry):
-        terms[q // blocks, q % blocks] = (group[first[q]] * has[q]).astype(terms.dtype)
+        terms[q // blocks, q % blocks] = jnp.where(has[q] != 0, group[first[q]], 0.0).astype(terms.dtype)
         return carry
 
     lax.fori_loop(0, terms.shape[0] * blocks, place, 0)
+
+
+def fill_tables(key, first, has):
+    n_tiles = key.shape[1]
+    for s in range(key.shape[0]):
+
+        def body(q, carry, s=s):
+            found = jnp.int32(0)
+            hit_any = jnp.int32(0)
+            for t in reversed(range(n_tiles)):
+                hit = key[s, t, 0] == q
+                found = jnp.where(hit, jnp.int32(t), found)
+                hit_any = jnp.where(hit, jnp.int32(1), hit_any)
+            first[s, q] = found
+            has[s, q] = hit_any
+            return carry
+
+        lax.fori_loop(0, first.shape[1], body, 0)
 
 
 def solve_kernel(plan, *refs):
     refs = list(refs)
-    (rhs, g_fwd, g_bwd, tiles, tiles_t, row_ids, col_ids,
-     fwd_first, fwd_has, bwd_first, bwd_has, out, prod, group) = [refs.pop(0) for _ in range(14)]
+    (rhs, diag, tiles, row_ids, col_ids, out, prod, group,
+     fwd_first, fwd_has, bwd_first, bwd_has) = [refs.pop(0) for _ in range(12)]
     bufs = []
     for ex, ga in plan:
         entry = {"work": (prod, group)}
@@ -142,6 +168,10 @@
 
     levels = tiles.shape[0]
 
+    def tables():
+        fill_tables(row_ids, fwd_first, fwd_has)
+        fill_tables(col_ids, bwd_first, bwd_has)
+
     def fwd_keys(s):
         return row_ids.at[s], fwd_first.at[s], fwd_has.at[s]
 
@@ -152,18 +182,18 @@
     for p, cfg in enumerate(plan):
         x = previous
         if p < levels:
-            phase(cfg, rhs.at[p], [g_fwd.at[p]], out.at[p], x, col_ids.at[p], tiles.at[p],
-                  fwd_keys(p), bufs[p])
+            phase(cfg, rhs.at[p], [(diag.at[p], True)], out.at[p], x, col_ids.at[p], tiles.at[p],
+                  fwd_keys(p), bufs[p], meanwhile=tables if p == 0 else None)
         elif p == levels:
-            phase(cfg, rhs.at[p], [g_fwd.at[p], g_bwd.at[p]], out.at[p], x, row_ids.at[p - 1],
-                  tiles_t.at[p - 1], bwd_keys(p - 1), bufs[p])
+            phase(cfg, rhs.at[p], [(diag.at[p], True), (diag.at[p], False)], out.at[p], x,
+                  row_ids.at[p - 1], tiles.at[p - 1], bwd_keys(p - 1), bufs[p], tiles_transposed=True)
         else:
             s = 2 * levels - p
             if s > 0:
-                phase(cfg, out.at[s], [g_bwd.at[s]], out.at[s], x, row_ids.at[s - 1], tiles_t.at[s - 1],
-                      bwd_keys(s - 1), bufs[p])
+                phase(cfg, out.at[s], [(diag.at[s], False)], out.at[s], x, row_ids.at[s - 1],
+                      tiles.at[s - 1], bwd_keys(s - 1), bufs[p], tiles_transposed=True)
             else:
-                phase(cfg, out.at[s], [g_bwd.at[s]], out.at[s], x, None, None, None, bufs[p])
+                phase(cfg, out.at[s], [(diag.at[s], False)], out.at[s], x, None, None, None, bufs[p])
         if cfg[1]:
             previous = bufs[p]["ga"][4]
 
@@ -173,20 +203,7 @@
     rows_dev = right_sides.shape[1]
     block = right_sides.shape[2]
     group_rows = rows_dev * n_row
-    row_ids = tile_row[:, :, 0]
-    col_ids = tile_col[:, :, 0]
-    split = diag_inverse.reshape(levels + 1, block, rows_dev, block)
-    g_fwd = split.transpose(0, 2, 3, 1)
-    g_bwd = split.transpose(0, 2, 1, 3)
-    tiles_t = jnp.swapaxes(factor_tiles, 2, 3)
     row_axis, col_axis = ("row", n_row), ("col", n_col)
-
-    def grouping(keys, size):
-        hits = keys[:, :, None] == jnp.arange(size, dtype=jnp.int32)[None, None, :]
-        return jnp.argmax(hits, axis=1).astype(jnp.int32), jnp.any(hits, axis=1).astype(jnp.float32)
-
-    fwd_first, fwd_has = grouping(row_ids, n_col * rows_dev)
-    bwd_first, bwd_has = grouping(col_ids, group_rows)
 
     plan = [(None, row_axis)]
     plan += [(col_axis, row_axis)] * (levels - 1)
@@ -201,6 +218,10 @@
     scratch = [
         pltpu.VMEM((n_tiles,) + piece[1:], jnp.float32),
         pltpu.VMEM((n_tiles,) + piece[1:], jnp.float32),
+        pltpu.SMEM((levels, n_col * rows_dev), jnp.int32),
+        pltpu.SMEM((levels, n_col * rows_dev), jnp.int32),
+        pltpu.SMEM((levels, group_rows), jnp.int32),
+        pltpu.SMEM((levels, group_rows), jnp.int32),
     ]
     for ex, ga in plan:
         if ex:
@@ -218,9 +239,8 @@
                 pltpu.SemaphoreType.DMA((rows_dev, ga[1])),
                 pltpu.VMEM((targets,) + piece, jnp.bfloat16),
             ]
-    args = [right_sides, g_fwd, g_bwd, factor_tiles, tiles_t, row_ids, col_ids,
-            fwd_first, fwd_has, bwd_first, bwd_has]
-    specs = [vmem] * 5 + [smem] * 6
+    args = [right_sides, diag_inverse, factor_tiles, tile_row, tile_col]
+    specs = [vmem] * 3 + [smem] * 2
     return pl.pallas_call(
         functools.partial(solve_kernel, plan),
         out_shape=jax.ShapeDtypeStruct(right_sides.shape, jnp.float32),

time: 169 us -> 167 us (0.988)
  Pallas kernels: 160 us -> 163 us
  other arithmetic: 2.7 us -> 0 us
  local copies, waits for them, and re-layouts: 6.06 us -> 3.77 us
    reshape x3 -> x0, local copies, waits for them, and re-layouts: 2.64 us -> none  [solve_all(): split = diag_inverse.reshape(levels + 1, block, rows_dev, block)]
    pallas_call x1, Pallas kernels: 160 us -> 163 us  [solve_all(): pl.pallas_call(functools.partial(solve_kernel, plan), out_shape=jax.Shape...]
    unnamed x9 -> x5, local copies, waits for them, and re-layouts: 3.42 us -> 3.77 us
where the time goes in v7:
time: 167 us; the launch traced here: 166 us
  Pallas kernels  163 us (98%)
  local copies, waits for them, and re-layouts  3.77 us (2%)
    pallas_call x1, Pallas kernels, solve_all(): pl.pallas_call(functools.partial(solve_kernel, plan), out_shape=jax.Shape...  163 us
    unnamed x5, local copies, waits for them, and re-layouts  3.77 us

profile of v7, /device:TPU:1, one launch (start us, length us, event | category | flops | bytes accessed | tf_op | source)
XLA Modules:
  0.0 166.5 jit_solution(3243202499325670808)
XLA Ops:
  0.0 0.0 copy-start
  0.0 1.4 copy.6.refs_3_
  1.4 0.0 copy-done
  1.4 0.7 copy.7.refs_4_
  2.1 162.7 %shard_map.55 = f32[4,2,64,128]{3,2,1,0:T(8,128)} custom-call(f32[4,2,64,128]{3,2,1,0:T(8,128)} %refs_0_.1, f32[4,64,128]{2,1,0:T(8,128)} %refs_1_.1, bf16[3,12,64,64]{3,2,1,0:T(8,128)(2,1)} %refs_2_.1, s32[3,12,1]{2,1,0:T(8,128)} %copy.6.refs_3_, s32[3,12,1]{2,1,0:T(8,128)} %copy.7.refs_4_), custom_call_target="tpu_custom_call" | custom-call | tf_op jit(solution)/shard_map/pallas_call | solution.py:244
  164.8 1.7 %copy.9 = f32[4,2,64,128]{3,2,1,0:T(8,128)} copy(f32[4,2,64,128]{3,2,1,0:T(8,128)} %shard_map.55) | data formatting | bytes 524288
Async XLA Ops:
  0.0 1.4 copy-start

commit v8 on v7

--- a/solution.py
+++ b/solution.py
@@ -12,6 +12,13 @@
 HIGHEST = lax.Precision.HIGHEST
 
 
+def offsets(n):
+    out = []
+    for d in range(1, n // 2 + 1):
+        out += [d] if 2 * d == n else [d, n - d]
+    return out
+
+
 def peer_id(axis, peer):
     return tuple(peer if name == axis else lax.axis_index(name) for name in AXES)
 
@@ -25,8 +32,8 @@
         held_x, ex_send, ex_recv = bufs["ex"]
         me = lax.axis_index(axis)
         copies = []
-        for k in range(1, n):
-            peer = lax.rem(me + k, n)
+        for k, d in enumerate(offsets(n), start=1):
+            peer = lax.rem(me + d, n)
             copy = pltpu.make_async_remote_copy(
                 src_ref=x.at[peer, kb],
                 dst_ref=held_x.at[k, kb],
@@ -72,8 +79,8 @@
             held_g, stage, ga_send, ga_recv, _ = bufs["ga"]
             me = lax.axis_index(axis)
             stage[kb] = value.astype(stage.dtype)
-            for k in range(1, n):
-                peer = lax.rem(me + k, n)
+            for k, d in enumerate(offsets(n), start=1):
+                peer = lax.rem(me + d, n)
                 copy = pltpu.make_async_remote_copy(
                     src_ref=stage.at[kb],
                     dst_ref=held_g.at[me * blocks + kb],
@@ -97,7 +104,7 @@
 
     def product(t, carry):
         contract = 0 if tiles_transposed else 1
-        prod[t] = lax.dot_general(tiles[t], held_g[ids[t, 0]], (((contract,), (0,)), ((), ())),
+        prod[t] = lax.dot_general(tiles[t], held_g[ids[t]], (((contract,), (0,)), ((), ())),
                                   preferred_element_type=jnp.float32)
         return carry
 
@@ -105,10 +112,10 @@
     key, first, has = keys
 
     def grouping(t, carry):
-        mine = key[t, 0]
+        mine = key[t]
         acc = jnp.zeros(prod.shape[1:], jnp.float32)
         for other in range(n_tiles):
-            acc = acc + jnp.where(key[other, 0] == mine, prod[other], 0.0)
+            acc = acc + jnp.where(key[other] == mine, prod[other], 0.0)
         group[t] = acc
         return carry
 
@@ -129,7 +136,7 @@
             found = jnp.int32(0)
             hit_any = jnp.int32(0)
             for t in reversed(range(n_tiles)):
-                hit = key[s, t, 0] == q
+                hit = key[s, t] == q
                 found = jnp.where(hit, jnp.int32(t), found)
                 hit_any = jnp.where(hit, jnp.int32(1), hit_any)
             first[s, q] = found
@@ -239,7 +246,8 @@
                 pltpu.SemaphoreType.DMA((rows_dev, ga[1])),
                 pltpu.VMEM((targets,) + piece, jnp.bfloat16),
             ]
-    args = [right_sides, diag_inverse, factor_tiles, tile_row, tile_col]
+    ids = [tile_row.reshape(tile_row.shape[:2]), tile_col.reshape(tile_col.shape[:2])]
+    args = [right_sides, diag_inverse, factor_tiles] + ids
     specs = [vmem] * 3 + [smem] * 2
     return pl.pallas_call(
         functools.partial(solve_kernel, plan),

time: 167 us -> 167 us (level)
    unnamed x5 -> x2, local copies, waits for them, and re-layouts: 3.77 us -> 2.95 us
where the time goes in v8:
time: 167 us
  Pallas kernels  164 us (98%)
  local copies, waits for them, and re-layouts  2.95 us (2%)
    pallas_call x1, Pallas kernels, solve_all(): pl.pallas_call(functools.partial(solve_kernel, plan), out_shape=jax.Shape...  164 us

profile of v8, /device:TPU:1, one launch (start us, length us, event | category | flops | bytes accessed | tf_op | source)
XLA Modules:
  0.0 167.2 jit_solution(606607795698624731)
XLA Ops:
  0.0 1.3 copy_bitcast_fusion
  1.3 164.2 %shard_map.55 = f32[4,2,64,128]{3,2,1,0:T(8,128)} custom-call(f32[4,2,64,128]{3,2,1,0:T(8,128)} %refs_0_.1, f32[4,64,128]{2,1,0:T(8,128)} %refs_1_.1, bf16[3,12,64,64]{3,2,1,0:T(8,128)(2,1)} %refs_2_.1, s32[3,12]{1,0:T(4,128)} %get-tuple-element.6.refs_3_, s32[3,12]{1,0:T(4,128)} %get-tuple-element.5.refs_4_), custom_call_target="tpu_custom_call" | custom-call | tf_op jit(solution)/shard_map/pallas_call | solution.py:252
  165.5 1.7 copy.11

commit v9 on v8

--- a/solution.py
+++ b/solution.py
@@ -12,13 +12,6 @@
 HIGHEST = lax.Precision.HIGHEST
 
 
-def offsets(n):
-    out = []
-    for d in range(1, n // 2 + 1):
-        out += [d] if 2 * d == n else [d, n - d]
-    return out
-
-
 def peer_id(axis, peer):
     return tuple(peer if name == axis else lax.axis_index(name) for name in AXES)
 
@@ -32,7 +25,7 @@
         held_x, ex_send, ex_recv = bufs["ex"]
         me = lax.axis_index(axis)
         copies = []
-        for k, d in enumerate(offsets(n), start=1):
+        for k, d in enumerate(range(1, n), start=1):
             peer = lax.rem(me + d, n)
             copy = pltpu.make_async_remote_copy(
                 src_ref=x.at[peer, kb],
@@ -79,7 +72,7 @@
             held_g, stage, ga_send, ga_recv, _ = bufs["ga"]
             me = lax.axis_index(axis)
             stage[kb] = value.astype(stage.dtype)
-            for k, d in enumerate(offsets(n), start=1):
+            for k, d in enumerate(range(1, n), start=1):
                 peer = lax.rem(me + d, n)
                 copy = pltpu.make_async_remote_copy(
                     src_ref=stage.at[kb],

time: 167 us -> 165 us (0.988)
  Pallas kernels: 164 us -> 162 us
    pallas_call x1, Pallas kernels: 164 us -> 162 us  [solve_all(): pl.pallas_call(functools.partial(solve_kernel, plan), out_shape=jax.Shape...]
where the time goes in v9:
time: 165 us
  Pallas kernels  162 us (98%)
  local copies, waits for them, and re-layouts  2.95 us (2%)
    pallas_call x1, Pallas kernels, solve_all(): pl.pallas_call(functools.partial(solve_kernel, plan), out_shape=jax.Shape...  162 us

profile of v9, /device:TPU:1, one launch (start us, length us, event | category | flops | bytes accessed | tf_op | source)
XLA Modules:
  0.0 165.2 jit_solution(7134439521762087050)
XLA Ops:
  0.0 1.3 copy_bitcast_fusion
  1.3 162.3 %shard_map.55 = f32[4,2,64,128]{3,2,1,0:T(8,128)} custom-call(f32[4,2,64,128]{3,2,1,0:T(8,128)} %refs_0_.1, f32[4,64,128]{2,1,0:T(8,128)} %refs_1_.1, bf16[3,12,64,64]{3,2,1,0:T(8,128)(2,1)} %refs_2_.1, s32[3,12]{1,0:T(4,128)} %get-tuple-element.6.refs_3_, s32[3,12]{1,0:T(4,128)} %get-tuple-element.5.refs_4_), custom_call_target="tpu_custom_call" | custom-call | tf_op jit(solution)/shard_map/pallas_call | solution.py:245
  163.5 1.7 %copy.11 = f32[4,2,64,128]{3,2,1,0:T(8,128)} copy(f32[4,2,64,128]{3,2,1,0:T(8,128)} %shard_map.55) | data formatting | bytes 524288

commit v10 on v9

--- a/solution.py
+++ b/solution.py
@@ -142,7 +142,7 @@
 def solve_kernel(plan, *refs):
     refs = list(refs)
     (rhs, diag, tiles, row_ids, col_ids, out, prod, group,
-     fwd_first, fwd_has, bwd_first, bwd_has) = [refs.pop(0) for _ in range(12)]
+     fwd_first, fwd_has, bwd_first, bwd_has, tiles_t) = [refs.pop(0) for _ in range(13)]
     bufs = []
     for ex, ga in plan:
         entry = {"work": (prod, group)}
@@ -171,6 +171,9 @@
     def tables():
         fill_tables(row_ids, fwd_first, fwd_has)
         fill_tables(col_ids, bwd_first, bwd_has)
+        for s in range(levels):
+            for t in range(tiles.shape[1]):
+                tiles_t[s, t] = tiles[s, t].T
 
     def fwd_keys(s):
         return row_ids.at[s], fwd_first.at[s], fwd_has.at[s]
@@ -186,12 +189,12 @@
                   fwd_keys(p), bufs[p], meanwhile=tables if p == 0 else None)
         elif p == levels:
             phase(cfg, rhs.at[p], [(diag.at[p], True), (diag.at[p], False)], out.at[p], x,
-                  row_ids.at[p - 1], tiles.at[p - 1], bwd_keys(p - 1), bufs[p], tiles_transposed=True)
+                  row_ids.at[p - 1], tiles_t.at[p - 1], bwd_keys(p - 1), bufs[p])
         else:
             s = 2 * levels - p
             if s > 0:
                 phase(cfg, out.at[s], [(diag.at[s], False)], out.at[s], x, row_ids.at[s - 1],
-                      tiles.at[s - 1], bwd_keys(s - 1), bufs[p], tiles_transposed=True)
+                      tiles_t.at[s - 1], bwd_keys(s - 1), bufs[p])
             else:
                 phase(cfg, out.at[s], [(diag.at[s], False)], out.at[s], x, None, None, None, bufs[p])
         if cfg[1]:
@@ -222,6 +225,7 @@
         pltpu.SMEM((levels, n_col * rows_dev), jnp.int32),
         pltpu.SMEM((levels, group_rows), jnp.int32),
         pltpu.SMEM((levels, group_rows), jnp.int32),
+        pltpu.VMEM(factor_tiles.shape, factor_tiles.dtype),
     ]
     for ex, ga in plan:
         if ex:

time: 165 us -> 164 us (level)
  Pallas kernels: 162 us -> 160 us
    pallas_call x1, Pallas kernels: 162 us -> 160 us  [solve_all(): pl.pallas_call(functools.partial(solve_kernel, plan), out_shape=jax.Shape...]
where the time goes in v10:
time: 164 us; the launch traced here: 163 us
  Pallas kernels  160 us (98%)
  local copies, waits for them, and re-layouts  2.95 us (2%)
    pallas_call x1, Pallas kernels, solve_all(): pl.pallas_call(functools.partial(solve_kernel, plan), out_shape=jax.Shape...  160 us

profile of v10, /device:TPU:1, one launch (start us, length us, event | category | flops | bytes accessed | tf_op | source)
XLA Modules:
  0.0 163.4 jit_solution(4242401286643115866)
XLA Ops:
  0.0 1.3 copy_bitcast_fusion
  1.3 160.4 %shard_map.55 = f32[4,2,64,128]{3,2,1,0:T(8,128)} custom-call(f32[4,2,64,128]{3,2,1,0:T(8,128)} %refs_0_.1, f32[4,64,128]{2,1,0:T(8,128)} %refs_1_.1, bf16[3,12,64,64]{3,2,1,0:T(8,128)(2,1)} %refs_2_.1, s32[3,12]{1,0:T(4,128)} %get-tuple-element.6.refs_3_, s32[3,12]{1,0:T(4,128)} %get-tuple-element.5.refs_4_), custom_call_target="tpu_custom_call" | custom-call | tf_op jit(solution)/shard_map/pallas_call | solution.py:249
  161.7 1.7 %copy.11 = f32[4,2,64,128]{3,2,1,0:T(8,128)} copy(f32[4,2,64,128]{3,2,1,0:T(8,128)} %shard_map.55) | data formatting | bytes 524288

commit v11 on v10

--- a/solution.py
+++ b/solution.py
@@ -62,8 +62,11 @@
             value = value - total
         width = value.shape[0]
         for diag, transposed in gs:
-            d = diag[:, pl.ds(kb * width, width)]
-            contract = 0 if transposed else 1
+            if transposed is None:
+                d, contract = diag[kb], 1
+            else:
+                d = diag[:, pl.ds(kb * width, width)]
+                contract = 0 if transposed else 1
             value = lax.dot_general(d, value, (((contract,), (0,)), ((), ())),
                                     precision=HIGHEST, preferred_element_type=jnp.float32)
         out[kb] = value
@@ -142,7 +145,7 @@
 def solve_kernel(plan, *refs):
     refs = list(refs)
     (rhs, diag, tiles, row_ids, col_ids, out, prod, group,
-     fwd_first, fwd_has, bwd_first, bwd_has, tiles_t) = [refs.pop(0) for _ in range(13)]
+     fwd_first, fwd_has, bwd_first, bwd_has, tiles_t, g_fwd) = [refs.pop(0) for _ in range(14)]
     bufs = []
     for ex, ga in plan:
         entry = {"work": (prod, group)}
@@ -174,6 +177,10 @@
         for s in range(levels):
             for t in range(tiles.shape[1]):
                 tiles_t[s, t] = tiles[s, t].T
+        width = g_fwd.shape[-1]
+        for s in range(1, levels + 1):
+            for kb in range(g_fwd.shape[1]):
+                g_fwd[s, kb] = diag[s, :, pl.ds(kb * width, width)].T
 
     def fwd_keys(s):
         return row_ids.at[s], fwd_first.at[s], fwd_has.at[s]
@@ -185,10 +192,11 @@
     for p, cfg in enumerate(plan):
         x = previous
         if p < levels:
-            phase(cfg, rhs.at[p], [(diag.at[p], True)], out.at[p], x, col_ids.at[p], tiles.at[p],
+            g = (diag.at[p], True) if p == 0 else (g_fwd.at[p], None)
+            phase(cfg, rhs.at[p], [g], out.at[p], x, col_ids.at[p], tiles.at[p],
                   fwd_keys(p), bufs[p], meanwhile=tables if p == 0 else None)
         elif p == levels:
-            phase(cfg, rhs.at[p], [(diag.at[p], True), (diag.at[p], False)], out.at[p], x,
+            phase(cfg, rhs.at[p], [(g_fwd.at[p], None), (diag.at[p], False)], out.at[p], x,
                   row_ids.at[p - 1], tiles_t.at[p - 1], bwd_keys(p - 1), bufs[p])
         else:
             s = 2 * levels - p
@@ -226,6 +234,7 @@
         pltpu.SMEM((levels, group_rows), jnp.int32),
         pltpu.SMEM((levels, group_rows), jnp.int32),
         pltpu.VMEM(factor_tiles.shape, factor_tiles.dtype),
+        pltpu.VMEM((levels + 1, rows_dev, block, block), jnp.float32),
     ]
     for ex, ga in plan:
         if ex:

time: 164 us -> 163 us (level)
  no operation moved by 1% of the time
where the time goes in v11:
time: 163 us
  Pallas kernels  160 us (98%)
  local copies, waits for them, and re-layouts  2.95 us (2%)
    pallas_call x1, Pallas kernels, solve_all(): pl.pallas_call(functools.partial(solve_kernel, plan), out_shape=jax.Shape...  160 us

profile of v11, /device:TPU:1, one launch (start us, length us, event | category | flops | bytes accessed | tf_op | source)
XLA Modules:
  0.0 163.1 jit_solution(8038093373068886052)
XLA Ops:
  0.0 1.3 copy_bitcast_fusion
  1.3 160.2 %shard_map.55 = f32[4,2,64,128]{3,2,1,0:T(8,128)} custom-call(f32[4,2,64,128]{3,2,1,0:T(8,128)} %refs_0_.1, f32[4,64,128]{2,1,0:T(8,128)} %refs_1_.1, bf16[3,12,64,64]{3,2,1,0:T(8,128)(2,1)} %refs_2_.1, s32[3,12]{1,0:T(4,128)} %get-tuple-element.6.refs_3_, s32[3,12]{1,0:T(4,128)} %get-tuple-element.5.refs_4_), custom_call_target="tpu_custom_call" | custom-call | tf_op jit(solution)/shard_map/pallas_call | solution.py:258
  161.4 1.7 %copy.11 = f32[4,2,64,128]{3,2,1,0:T(8,128)} copy(f32[4,2,64,128]{3,2,1,0:T(8,128)} %shard_map.55) | data formatting | bytes 524288

commit v12 on v11

--- a/solution.py
+++ b/solution.py
@@ -104,7 +104,7 @@
                                   preferred_element_type=jnp.float32)
         return carry
 
-    lax.fori_loop(0, n_tiles, product, 0)
+    lax.fori_loop(0, n_tiles, product, 0, unroll=True)
     key, first, has = keys
 
     def grouping(t, carry):
@@ -115,7 +115,7 @@
         group[t] = acc
         return carry
 
-    lax.fori_loop(0, n_tiles, grouping, 0)
+    lax.fori_loop(0, n_tiles, grouping, 0, unroll=True)
 
     def place(q, carry):
         terms[q // blocks, q % blocks] = jnp.where(has[q] != 0, group[first[q]], 0.0).astype(terms.dtype)

time: 163 us -> 156 us (0.957)
  Pallas kernels: 160 us -> 152 us
    pallas_call x1, Pallas kernels: 160 us -> 152 us  [solve_all(): pl.pallas_call(functools.partial(solve_kernel, plan), out_shape=jax.Shape...]
where the time goes in v12:
time: 156 us; the launch traced here: 155 us
  Pallas kernels  152 us (97%)
  local copies, waits for them, and re-layouts  2.95 us (2%)
    pallas_call x1, Pallas kernels, solve_all(): pl.pallas_call(functools.partial(solve_kernel, plan), out_shape=jax.Shape...  152 us

profile of v12, /device:TPU:1, one launch (start us, length us, event | category | flops | bytes accessed | tf_op | source)
XLA Modules:
  0.0 155.4 jit_solution(3913651052950104324)
XLA Ops:
  0.0 1.3 copy_bitcast_fusion
  1.3 152.5 %shard_map.55 = f32[4,2,64,128]{3,2,1,0:T(8,128)} custom-call(f32[4,2,64,128]{3,2,1,0:T(8,128)} %refs_0_.1, f32[4,64,128]{2,1,0:T(8,128)} %refs_1_.1, bf16[3,12,64,64]{3,2,1,0:T(8,128)(2,1)} %refs_2_.1, s32[3,12]{1,0:T(4,128)} %get-tuple-element.6.refs_3_, s32[3,12]{1,0:T(4,128)} %get-tuple-element.5.refs_4_), custom_call_target="tpu_custom_call" | custom-call | tf_op jit(solution)/shard_map/pallas_call | solution.py:258
  153.7 1.7 %copy.11 = f32[4,2,64,128]{3,2,1,0:T(8,128)} copy(f32[4,2,64,128]{3,2,1,0:T(8,128)} %shard_map.55) | data formatting | bytes 524288

commit v13 on v12

--- a/solution.py
+++ b/solution.py
@@ -121,7 +121,7 @@
         terms[q // blocks, q % blocks] = jnp.where(has[q] != 0, group[first[q]], 0.0).astype(terms.dtype)
         return carry
 
-    lax.fori_loop(0, terms.shape[0] * blocks, place, 0)
+    lax.fori_loop(0, terms.shape[0] * blocks, place, 0, unroll=True)
 
 
 def fill_tables(key, first, has):

time: 156 us -> 153 us (0.981)
  Pallas kernels: 152 us -> 149 us
    pallas_call x1, Pallas kernels: 152 us -> 149 us  [solve_all(): pl.pallas_call(functools.partial(solve_kernel, plan), out_shape=jax.Shape...]
where the time goes in v13:
time: 153 us; the launch traced here: 152 us
  Pallas kernels  149 us (97%)
  local copies, waits for them, and re-layouts  2.95 us (2%)
    pallas_call x1, Pallas kernels, solve_all(): pl.pallas_call(functools.partial(solve_kernel, plan), out_shape=jax.Shape...  149 us

profile of v13, /device:TPU:1, one launch (start us, length us, event | category | flops | bytes accessed | tf_op | source)
XLA Modules:
  0.0 152.4 jit_solution(3487604492313284404)
XLA Ops:
  0.0 1.3 copy_bitcast_fusion
  1.3 149.4 %shard_map.55 = f32[4,2,64,128]{3,2,1,0:T(8,128)} custom-call(f32[4,2,64,128]{3,2,1,0:T(8,128)} %refs_0_.1, f32[4,64,128]{2,1,0:T(8,128)} %refs_1_.1, bf16[3,12,64,64]{3,2,1,0:T(8,128)(2,1)} %refs_2_.1, s32[3,12]{1,0:T(4,128)} %get-tuple-element.6.refs_3_, s32[3,12]{1,0:T(4,128)} %get-tuple-element.5.refs_4_), custom_call_target="tpu_custom_call" | custom-call | tf_op jit(solution)/shard_map/pallas_call | solution.py:258
  150.7 1.7 %copy.11 = f32[4,2,64,128]{3,2,1,0:T(8,128)} copy(f32[4,2,64,128]{3,2,1,0:T(8,128)} %shard_map.55) | data formatting | bytes 524288
